TPU v7x, 256 devices: a whole 4x4x8 slice. The times are simulated.
256 devices in a mesh: row: 16 (over x_hi, z), col: 16 (over y, x_lo, core).
Axes of the slice: x: 4 (x_hi: 2, x_lo: 2; x = x_hi * 2 + x_lo), y: 4, z: 8, core: 2. Of those that a mesh axis runs over, the one named last changes fastest.
Arguments:
- obj_re: float32 [2048, 2048], P('row', 'col'), may hold values from -6 to 6
- obj_im: float32 [2048, 2048], P('row', 'col'), may hold values from -6 to 6
- probe_re: float32 [4, 256, 256], replicated, may hold values from -3 to 3
- probe_im: float32 [4, 256, 256], replicated, may hold values from -3 to 3
- amps: float32 [16, 16, 1, 256, 256], P('row', 'col'), may hold values from 0.2 to 4
- positions: int32 [16, 16, 1, 2], P('row', 'col'), may hold values from -128 to 1920, as said below
Outputs:
- new_obj_re: float32 [2048, 2048], P('row', 'col')
- new_obj_im: float32 [2048, 2048], P('row', 'col')
- new_probe_re: float32 [4, 256, 256], replicated
- new_probe_im: float32 [4, 256, 256], replicated
Inputs may be any that keep to these rules, and one draw needn't show every extreme that they name: `positions`: each position's offsets are multiples of 64. A position stored at [i, j, p] has its row r with i * 128 - 256 // 2 <= r <= (i + 1) * 128 - 256 // 2 and its column c with j * 128 - 256 // 2 <= c <= (j + 1) * 128 - 256 // 2.
All inputs are finite; a program needn't handle non-finite values.
Results may differ from a plain program's by a relative error of at most 0.0055.
Values sent between devices are 32-bit elements; how exact they have to be, the bound alone decides.
A program may use at most 64 MiB of HBM per device.

v0:
```python
import math

import jax
import jax.numpy as jnp
from jax import lax
from jax.sharding import PartitionSpec as P

ITERS = 3


amp_floor = 0.25
light_ratio = 0.1
mass_ratio = 0.1
probe_step = 6.0


def passed_along(array, axis, by):
    devices = lax.axis_size(axis)
    pairs = [(i, i + by) for i in range(devices) if 0 <= i + by < devices]
    return lax.ppermute(array, axis, pairs)


def with_halo(cells, sides, width):
    for axis, dim in sides:
        count = lax.axis_size(axis)
        ends = count - 1
        head = lax.slice_in_dim(cells, 0, width, axis=dim)
        tail = lax.slice_in_dim(cells, cells.shape[dim] - width, cells.shape[dim], axis=dim)
        cells = jnp.concatenate(
            [
                lax.ppermute(tail, axis, [(i, (i + 1) % count) for i in range(ends)]),
                cells,
                lax.ppermute(head, axis, [((i + 1) % count, i) for i in range(ends)]),
            ],
            axis=dim,
        )
    return cells


def make_tables(width, sign):
    index = jnp.arange(width, dtype=jnp.int32)
    turns = index[:, None] * index[None, :] % width
    angle = turns.astype(jnp.float32) * (2.0 * math.pi / width)
    real = (jnp.cos(angle) / math.sqrt(width)).astype(jnp.bfloat16)
    imag = (sign * jnp.sin(angle) / math.sqrt(width)).astype(jnp.bfloat16)
    right_pair = jnp.concatenate(
        [jnp.concatenate([real, imag], 1), jnp.concatenate([-imag, real], 1)], 0
    )
    return (right_pair, real, imag)


def transform(wave, table):
    right_pair, real, imag = table
    width = real.shape[0]
    half = jnp.einsum("mnc,cd->mnd", wave, right_pair, preferred_element_type=jnp.float32).astype(
        jnp.bfloat16
    )
    first = jnp.einsum("kn,mnd->mkd", real, half, preferred_element_type=jnp.float32)
    second = jnp.einsum("kn,mnd->mkd", imag, half, preferred_element_type=jnp.float32)
    return (first[..., :width] - second[..., width:], first[..., width:] + second[..., :width])


def one_view(window, probe_re, probe_im, view, forward, backward):
    win_re = window[0][None]
    win_im = window[1][None]
    psi = jnp.concatenate(
        [probe_re * win_re - probe_im * win_im, probe_re * win_im + probe_im * win_re], axis=2
    ).astype(jnp.bfloat16)
    spec_re, spec_im = transform(psi, forward)
    modulus = jnp.sqrt(jnp.sum(spec_re * spec_re + spec_im * spec_im, axis=0))
    factor = view / jnp.maximum(modulus, amp_floor) - 1.0
    change = jnp.concatenate([spec_re * factor, spec_im * factor], axis=2).astype(jnp.bfloat16)
    return transform(change, backward)


def place(buffer, piece, row_at, col_at):
    start = (jnp.int32(0), row_at, col_at)
    return lax.dynamic_update_slice(buffer, piece, start)


def send_rows(strip, offset):
    return passed_along(strip, "row", offset)


def send_cols(strip, offset):
    return passed_along(strip, "col", offset)


def fold_back(buffer, rows, cols, rim):
    middle = buffer[:, rim : rim + rows]
    from_below = send_rows(buffer[:, :rim], -1)
    from_above = send_rows(buffer[:, rim + rows :], 1)
    middle = middle.at[:, rows - rim :].add(from_below)
    middle = middle.at[:, :rim].add(from_above)
    core = middle[:, :, rim : rim + cols]
    from_right = send_cols(middle[:, :, :rim], -1)
    from_left = send_cols(middle[:, :, rim + cols :], 1)
    core = core.at[:, :, cols - rim :].add(from_right)
    return core.at[:, :, :rim].add(from_left)


def local(obj_re, obj_im, probe_re, probe_im, amps, positions):
    rows, cols = obj_re.shape
    modes, width = (probe_re.shape[0], probe_re.shape[1])
    rim = width // 2
    forward = make_tables(width, -1.0)
    backward = make_tables(width, 1.0)
    spots = positions[0, 0]
    views = amps[0, 0]
    my_row = lax.axis_index("row")
    my_col = lax.axis_index("col")
    row_base = my_row * rows - rim
    col_base = my_col * cols - rim
    local_rows = spots[:, 0] - row_base
    local_cols = spots[:, 1] - col_base
    wide_rows = rows + 2 * rim
    wide_cols = cols + 2 * rim
    power = jnp.sum(probe_re * probe_re + probe_im * probe_im, axis=0)
    light_buf = jnp.zeros((1, wide_rows, wide_cols), jnp.float32)
    slot = 0
    light_buf = place(light_buf, power[None], local_rows[slot], local_cols[slot])
    light = fold_back(light_buf, rows, cols, rim)[0]
    peak = lax.pmax(jnp.max(light), ("row", "col"))
    denom = light + light_ratio * peak
    state = jnp.stack([obj_re, obj_im])
    grad_re = jnp.zeros((modes, width, width), jnp.float32)
    grad_im = jnp.zeros((modes, width, width), jnp.float32)
    mass = jnp.zeros((width, width), jnp.float32)
    for step in range(ITERS):
        extended = with_halo(state, (("row", 1), ("col", 2)), rim)
        buffer = jnp.zeros((2, wide_rows, wide_cols), jnp.float32)
        last_pass = step == ITERS - 1
        slot = 0
        window = lax.dynamic_slice(
            extended, (jnp.int32(0), local_rows[slot], local_cols[slot]), (2, width, width)
        )
        exit_re, exit_im = one_view(window, probe_re, probe_im, views[slot], forward, backward)
        obj_grad = jnp.stack(
            [
                jnp.sum(probe_re * exit_re + probe_im * exit_im, axis=0),
                jnp.sum(probe_re * exit_im - probe_im * exit_re, axis=0),
            ]
        )
        buffer = place(buffer, obj_grad, local_rows[slot], local_cols[slot])
        if last_pass:
            win_re = window[0][None]
            win_im = window[1][None]
            grad_re = win_re * exit_re + win_im * exit_im
            grad_im = win_re * exit_im - win_im * exit_re
            mass = window[0] * window[0] + window[1] * window[1]
        state = state + fold_back(buffer, rows, cols, rim) / denom[None]
    pixels = width * width
    terms = jnp.concatenate(
        [grad_re.reshape(modes, pixels), grad_im.reshape(modes, pixels), mass.reshape(1, pixels)],
        axis=0,
    )
    probe_flat = jnp.concatenate(
        [probe_re.reshape(modes, pixels), probe_im.reshape(modes, pixels)], axis=0
    )
    summed = lax.psum(terms, ("row", "col"))
    scale = probe_step / (summed[2 * modes] + mass_ratio * jnp.mean(summed[2 * modes]))
    updated = probe_flat + summed[: 2 * modes] * scale[None]
    new_re = updated[:modes].reshape(modes, width, width)
    new_im = updated[modes:].reshape(modes, width, width)
    return (state[0], state[1], new_re, new_im)


def solution(mesh):
    placed = (
        P("row", "col"),
        P("row", "col"),
        P(),
        P(),
        P("row", "col", None, None, None),
        P("row", "col", None, None),
    )
    return jax.shard_map(
        local,
        mesh=mesh,
        in_specs=placed,
        out_specs=(P("row", "col"), P("row", "col"), P(), P()),
        check_vma=False,
    )
```

profile of v0, /device:TPU:1, one launch (start us, length us, event | category | flops | bytes accessed | tf_op | source)
XLA Modules:
  0.0 618.5 jit_solution(10108683802256742106)
XLA Ops:
  8.3 4.4 collective-permute-start
  13.9 1.6 fusion.77
  15.6 3.4 collective-permute-done.1
  19.0 1.7 pad_maximum_fusion.8
  20.7 4.7 collective-permute-start.2
  25.3 1.9 collective-permute-start.3
  34.7 1.6 multiply_convert_fusion.7
  36.4 1.8 fusion.32
  40.1 1.4 convolution_bitcast_fusion.10
  41.5 1.4 convolution_bitcast_fusion.11
  44.5 2.8 convolution_bitcast_fusion.8
  47.3 2.7 convolution_bitcast_fusion.9
  50.8 3.6 dynamic_update_slice.13
  54.4 1.8 fusion.151
  57.5 4.7 collective-permute-start.9
  62.2 3.0 add_reduce_fusion.5
  66.1 2.1 copy.48
  69.3 6.1 dynamic_update_slice.12
  75.4 2.1 fusion.150
  78.7 4.8 collective-permute-start.5
  84.7 1.9 collective-permute-start.10
  86.6 3.6 collective-permute-start.11
  92.2 89.7 %pmax.7 = f32[]{:T(128)} all-reduce(f32[]{:T(128)} %fusion.146), channel_id=1, replica_groups=mesh['row'=16,'col'=16] {'row','col'}, use_global_device_ids=true, to_apply=%region_5.6 | all-reduce | flops 1 | bytes 8 | tf_op jit(solution)/shard_map/pmax | solution.py:123
  183.9 3.1 collective-permute-start.6
  186.9 2.5 collective-permute-start.7
  192.3 1.7 collective-permute-start.12
  195.3 1.5 collective-permute-done.12
  196.8 4.2 collective-permute-done.13
  201.0 4.6 collective-permute-start.14
  205.6 1.9 collective-permute-start.15
  207.5 2.8 collective-permute-done.14
  210.3 5.4 collective-permute-done.15
  218.1 1.4 convolution_bitcast_fusion.6
  219.5 1.4 convolution_bitcast_fusion.7
  223.1 1.4 convolution_bitcast_fusion.4
  224.5 1.4 convolution_bitcast_fusion.5
  227.5 7.3 %dynamic_update_slice.14 = f32[2,384,384]{2,1,0:T(8,128)S(1)} dynamic-update-slice(f32[2,384,384]{2,1,0:T(8,128)S(1)} %broadcast.616.clone.1, f32[2,256,256]{2,1,0:T(8,128)} %copy.58, s32[]{:T(128)} %constant.547.clone.1, s32[]{:T(128)S(6)} %select_n.65, s32[]{:T(128)S(6)} %select_n.66) | dynamic-update-slice | bytes 1048580 | tf_op jit(solution)/shard_map/dynamic_update_slice | solution.py:78
  236.2 4.0 collective-permute-start.17
  240.3 3.2 collective-permute-done.16
  243.5 1.5 collective-permute-done.17
  245.0 1.9 collective-permute-start.18
  247.0 5.8 collective-permute-start.19
  253.5 4.2 collective-permute-done.19
  260.9 3.8 collective-permute-done.21
  264.7 5.9 collective-permute-start.22
  270.6 1.9 collective-permute-start.23
  272.5 3.3 collective-permute-done.22
  275.8 13.4 %collective-permute-done.23 = f32[2,384,128]{2,1,0:T(8,128)S(1)} collective-permute-done((f32[2,384,128]{2,1,0:T(8,128)S(1)}, f32[2,384,128]{2,1,0:T(8,128)S(1)}, u32[]{:S(2)}, u32[]{:S(2)}) %collective-permute-start.23) | collective-permute-done | bytes 393248 | tf_op jit(solution)/shard_map/ppermute | solution.py:33
  291.7 1.4 convolution_bitcast_fusion.2
  293.1 1.4 convolution_bitcast_fusion.3
  296.6 1.3 convolution_bitcast_fusion
  298.0 1.3 convolution_bitcast_fusion.1
  300.2 1.6 copy.86
  301.8 1.6 copy.85
  304.7 7.3 %dynamic_update_slice.15 = f32[2,384,384]{2,1,0:T(8,128)S(1)} dynamic-update-slice(f32[2,384,384]{2,1,0:T(8,128)S(1)} %broadcast.616, f32[2,256,256]{2,1,0:T(8,128)} %pad_maximum_fusion.7, s32[]{:T(128)} %constant.547.clone.1, s32[]{:T(128)S(6)} %select_n.65, s32[]{:T(128)S(6)} %select_n.66) | dynamic-update-slice | bytes 1048580 | tf_op jit(solution)/shard_map/dynamic_update_slice | solution.py:78
  314.3 5.0 collective-permute-start.25
  319.3 3.9 pad_maximum_fusion
  324.5 1.9 collective-permute-start.26
  326.4 5.0 collective-permute-start.27
  332.2 1.6 copy.84
  334.5 266.5 %all-reduce.2.cloned.1.call-done = f32[9,65536]{1,0:T(8,128)} async-done(((f32[9,65536]{1,0:T(8,128)}), f32[9,65536]{1,0:T(8,128)}) %all-reduce.2.cloned.1.call-update) | async-done | bytes 2359312 | tf_op jit(solution)/shard_map/psum | solution.py:160
  601.0 2.7 slice_reduce_fusion
  604.4 1.9 add_divide_fusion
  606.2 2.5 fusion
  (153 shorter events, 51.4 us)
Async XLA Ops:
  7.2 23.8 %copy-start = (f32[4,256,256]{2,1,0:T(8,128)S(1)}, f32[4,256,256]{2,1,0:T(8,128)}, u32[]{:S(2)}) copy-start(f32[4,256,256]{2,1,0:T(8,128)} %param.72) | copy-start | bytes 3145732
  7.2 24.2 %copy-start.1 = (f32[4,256,256]{2,1,0:T(8,128)S(1)}, f32[4,256,256]{2,1,0:T(8,128)}, u32[]{:S(2)}) copy-start(f32[4,256,256]{2,1,0:T(8,128)} %param.73) | copy-start | bytes 3145732
  7.2 593.8 %all-reduce.2.cloned.1.call-start = ((), (), s32[]{:S(2)}) async-start(), calls=%async_computation | async-start | bytes 8388608 | tf_op jit(solution)/shard_map/psum | solution.py:160
  8.3 7.3 %collective-permute-start = (f32[2,128,128]{2,1,0:T(8,128)S(1)}, f32[2,128,128]{2,1,0:T(8,128)S(1)}, u32[]{:S(2)}, u32[]{:S(2)}) collective-permute-start(f32[2,128,128]{2,1,0:T(8,128)S(1)} %pad_maximum_fusion.11), channel_id=1, source_target_pairs={{0,16},{16,32},{32,48},{48,64},{64,80},{80,96},{96,112},{112,128},... | collective-permute-start | bytes 393224 | tf_op jit(solution)/shard_map/ppermute | solution.py:31
  12.6 6.3 %collective-permute-start.1 = (f32[2,128,128]{2,1,0:T(8,128)S(1)}, f32[2,128,128]{2,1,0:T(8,128)S(1)}, u32[]{:S(2)}, u32[]{:S(2)}) collective-permute-start(f32[2,128,128]{2,1,0:T(8,128)S(1)} %pad_maximum_fusion.11), channel_id=1, source_target_pairs={{16,0},{32,16},{48,32},{64,48},{80,64},{96,80},{112,96},{128,112},... | collective-permute-start | bytes 393224 | tf_op jit(solution)/shard_map/ppermute | solution.py:33
  15.6 3.4 copy-start.14
  19.0 1.7 copy-start.15
  20.7 15.7 %collective-permute-start.2 = (f32[2,384,128]{2,1,0:T(8,128)}, f32[2,384,128]{2,1,0:T(8,128)}, u32[]{:S(2)}, u32[]{:S(2)}) collective-permute-start(f32[2,384,128]{2,1,0:T(8,128)} %pad_maximum_fusion.8), channel_id=1, source_target_pairs={{0,1},{1,2},{2,3},{3,4},{4,5},{5,6},{6,7},{7,8},{8,9},{9,10},{10,1... | collective-permute-start | bytes 1179656 | tf_op jit(solution)/shard_map/ppermute | solution.py:31
  25.3 11.0 %collective-permute-start.3 = (f32[2,384,128]{2,1,0:T(8,128)}, f32[2,384,128]{2,1,0:T(8,128)}, u32[]{:S(2)}, u32[]{:S(2)}) collective-permute-start(f32[2,384,128]{2,1,0:T(8,128)} %pad_maximum_fusion.8), channel_id=1, source_target_pairs={{1,0},{2,1},{3,2},{4,3},{5,4},{6,5},{7,6},{8,7},{9,8},{10,9},{11,1... | collective-permute-start | bytes 1179656 | tf_op jit(solution)/shard_map/ppermute | solution.py:33
  31.0 5.4 copy-start.9
  31.0 5.4 copy-start.10
  33.7 10.1 %copy-start.19 = (bf16[256,256]{1,0:T(8,128)(2,1)}, bf16[256,256]{1,0:T(8,128)(2,1)S(1)}, u32[]{:S(2)}) copy-start(bf16[256,256]{1,0:T(8,128)(2,1)S(1)} %fusion.78) | copy-start | bytes 393220
  34.7 9.1 %copy-start.22 = (bf16[256,256]{1,0:T(8,128)(2,1)}, bf16[256,256]{1,0:T(8,128)(2,1)S(1)}, u32[]{:S(2)}) copy-start(bf16[256,256]{1,0:T(8,128)(2,1)S(1)} %multiply_convert_fusion.6) | copy-start | bytes 393220
  36.3 3.0 copy-start.28
  36.3 7.4 %copy-start.25 = (bf16[256,256]{1,0:T(8,128)(2,1)}, bf16[256,256]{1,0:T(8,128)(2,1)S(1)}, u32[]{:S(2)}) copy-start(bf16[256,256]{1,0:T(8,128)(2,1)S(1)} %get-tuple-element.377) | copy-start | bytes 393220
  38.2 1.1 copy-start.16
  56.2 27.3 %collective-permute-start.8 = (f32[1,128,384]{2,1,0:T(8,128)}, f32[1,128,384]{2,1,0:T(8,128)}, u32[]{:S(2)}, u32[]{:S(2)}) collective-permute-start(f32[1,128,384]{2,1,0:T(8,128)} %get-tuple-element.355), channel_id=1, source_target_pairs={{16,0},{32,16},{48,32},{64,48},{80,64},{96,80},{112,96},{128,112},... | collective-permute-start | bytes 589832 | tf_op jit(solution)/shard_map/ppermute | solution.py:20
  57.5 26.0 %collective-permute-start.9 = (f32[1,128,384]{2,1,0:T(8,128)}, f32[1,128,384]{2,1,0:T(8,128)}, u32[]{:S(2)}, u32[]{:S(2)}) collective-permute-start(f32[1,128,384]{2,1,0:T(8,128)} %get-tuple-element.356), channel_id=1, source_target_pairs={{0,16},{16,32},{32,48},{48,64},{64,80},{80,96},{96,112},{112,128},... | collective-permute-start | bytes 589832 | tf_op jit(solution)/shard_map/ppermute | solution.py:20
  77.5 105.1 %collective-permute-start.4 = (f32[2,128,384]{2,1,0:T(8,128)}, f32[2,128,384]{2,1,0:T(8,128)}, u32[]{:S(2)}, u32[]{:S(2)}) collective-permute-start(f32[2,128,384]{2,1,0:T(8,128)} %get-tuple-element.353), channel_id=1, source_target_pairs={{16,0},{32,16},{48,32},{64,48},{80,64},{96,80},{112,96},{128,112},... | collective-permute-start | bytes 1179656 | tf_op jit(solution)/shard_map/ppermute | solution.py:20
  78.7 103.8 %collective-permute-start.5 = (f32[2,128,384]{2,1,0:T(8,128)}, f32[2,128,384]{2,1,0:T(8,128)}, u32[]{:S(2)}, u32[]{:S(2)}) collective-permute-start(f32[2,128,384]{2,1,0:T(8,128)} %get-tuple-element.354), channel_id=1, source_target_pairs={{0,16},{16,32},{32,48},{48,64},{64,80},{80,96},{96,112},{112,128},... | collective-permute-start | bytes 1179656 | tf_op jit(solution)/shard_map/ppermute | solution.py:20
  84.7 6.9 %copy-start.8 = (f32[1,128,384]{2,1,0:T(8,128)}, f32[1,128,384]{2,1,0:T(8,128)S(1)}, u32[]{:S(2)}) copy-start(f32[1,128,384]{2,1,0:T(8,128)S(1)} %fusion.48) | copy-start | bytes 589828
  84.7 5.6 collective-permute-start.10
  86.6 5.0 collective-permute-start.11
  183.9 6.5 %collective-permute-start.6 = (f32[2,128,128]{2,1,0:T(8,128)S(1)}, f32[2,128,128]{2,1,0:T(8,128)S(1)}, u32[]{:S(2)}, u32[]{:S(2)}) collective-permute-start(f32[2,128,128]{2,1,0:T(8,128)S(1)} %get-tuple-element.368), channel_id=1, source_target_pairs={{1,0},{2,1},{3,2},{4,3},{5,4},{6,5},{7,6},{8,7},{9,8},{10,9},{11,1... | collective-permute-start | bytes 393224 | tf_op jit(solution)/shard_map/ppermute | solution.py:20
  186.9 4.4 collective-permute-start.7
  190.3 6.5 %copy-start.11 = (f32[128,128]{1,0:T(8,128)}, f32[128,128]{1,0:T(8,128)S(1)}, u32[]{:S(2)}) copy-start(f32[128,128]{1,0:T(8,128)S(1)} %add_bitcast_fusion.2) | copy-start | bytes 196612
  192.3 24.4 %copy-start.6 = (f32[2,128,128]{2,1,0:T(8,128)}, f32[2,128,128]{2,1,0:T(8,128)S(1)}, u32[]{:S(2)}) copy-start(f32[2,128,128]{2,1,0:T(8,128)S(1)} %fusion.63) | copy-start | bytes 393220
  192.3 4.5 collective-permute-start.12
  194.0 6.9 %collective-permute-start.13 = (f32[2,128,128]{2,1,0:T(8,128)S(1)}, f32[2,128,128]{2,1,0:T(8,128)S(1)}, u32[]{:S(2)}, u32[]{:S(2)}) collective-permute-start(f32[2,128,128]{2,1,0:T(8,128)S(1)} %fusion.63), channel_id=1, source_target_pairs={{16,0},{32,16},{48,32},{64,48},{80,64},{96,80},{112,96},{128,112},... | collective-permute-start | bytes 393224 | tf_op jit(solution)/shard_map/ppermute | solution.py:33
  201.0 9.3 %collective-permute-start.14 = (f32[2,384,128]{2,1,0:T(8,128)S(1)}, f32[2,384,128]{2,1,0:T(8,128)S(1)}, u32[]{:S(2)}, u32[]{:S(2)}) collective-permute-start(f32[2,384,128]{2,1,0:T(8,128)S(1)} %pad_maximum_fusion.9), channel_id=1, source_target_pairs={{0,1},{1,2},{2,3},{3,4},{4,5},{5,6},{6,7},{7,8},{8,9},{9,10},{10,1... | collective-permute-start | bytes 1179656 | tf_op jit(solution)/shard_map/ppermute | solution.py:31
  205.6 10.1 %collective-permute-start.15 = (f32[2,384,128]{2,1,0:T(8,128)S(1)}, f32[2,384,128]{2,1,0:T(8,128)S(1)}, u32[]{:S(2)}, u32[]{:S(2)}) collective-permute-start(f32[2,384,128]{2,1,0:T(8,128)S(1)} %pad_maximum_fusion.9), channel_id=1, source_target_pairs={{1,0},{2,1},{3,2},{4,3},{5,4},{6,5},{7,6},{8,7},{9,8},{10,9},{11,1... | collective-permute-start | bytes 1179656 | tf_op jit(solution)/shard_map/ppermute | solution.py:33
  216.4 0.9 copy-start.17
  216.4 1.0 copy-start.26
  216.4 1.0 copy-start.29
  221.3 0.9 copy-start.20
  221.4 1.0 copy-start.23
  224.5 1.4 copy-start.2
  234.9 22.8 %copy-start.7 = (f32[2,128,128]{2,1,0:T(8,128)S(1)}, f32[2,128,128]{2,1,0:T(8,128)}, u32[]{:S(2)}) copy-start(f32[2,128,128]{2,1,0:T(8,128)} %copy-done.6) | copy-start | bytes 393220
  234.9 22.8 %copy-start.12 = (f32[128,128]{1,0:T(8,128)S(1)}, f32[128,128]{1,0:T(8,128)}, u32[]{:S(2)}) copy-start(f32[128,128]{1,0:T(8,128)} %copy-done.11) | copy-start | bytes 196612
  234.9 8.5 %collective-permute-start.16 = (f32[2,128,384]{2,1,0:T(8,128)S(1)}, f32[2,128,384]{2,1,0:T(8,128)S(1)}, u32[]{:S(2)}, u32[]{:S(2)}) collective-permute-start(f32[2,128,384]{2,1,0:T(8,128)S(1)} %get-tuple-element.351), channel_id=1, source_target_pairs={{16,0},{32,16},{48,32},{64,48},{80,64},{96,80},{112,96},{128,112},... | collective-permute-start | bytes 1179656 | tf_op jit(solution)/shard_map/ppermute | solution.py:20
  236.2 8.7 %collective-permute-start.17 = (f32[2,128,384]{2,1,0:T(8,128)S(1)}, f32[2,128,384]{2,1,0:T(8,128)S(1)}, u32[]{:S(2)}, u32[]{:S(2)}) collective-permute-start(f32[2,128,384]{2,1,0:T(8,128)S(1)} %get-tuple-element.352), channel_id=1, source_target_pairs={{0,16},{16,32},{32,48},{48,64},{64,80},{80,96},{96,112},{112,128},... | collective-permute-start | bytes 1179656 | tf_op jit(solution)/shard_map/ppermute | solution.py:20
  245.0 8.4 %collective-permute-start.18 = (f32[2,128,128]{2,1,0:T(8,128)S(1)}, f32[2,128,128]{2,1,0:T(8,128)S(1)}, u32[]{:S(2)}, u32[]{:S(2)}) collective-permute-start(f32[2,128,128]{2,1,0:T(8,128)S(1)} %get-tuple-element.366), channel_id=1, source_target_pairs={{1,0},{2,1},{3,2},{4,3},{5,4},{6,5},{7,6},{8,7},{9,8},{10,9},{11,1... | collective-permute-start | bytes 393224 | tf_op jit(solution)/shard_map/ppermute | solution.py:20
  247.0 10.7 %collective-permute-start.19 = (f32[2,128,128]{2,1,0:T(8,128)S(1)}, f32[2,128,128]{2,1,0:T(8,128)S(1)}, u32[]{:S(2)}, u32[]{:S(2)}) collective-permute-start(f32[2,128,128]{2,1,0:T(8,128)S(1)} %get-tuple-element.367), channel_id=1, source_target_pairs={{0,1},{1,2},{2,3},{3,4},{4,5},{5,6},{6,7},{7,8},{8,9},{9,10},{10,1... | collective-permute-start | bytes 393224 | tf_op jit(solution)/shard_map/ppermute | solution.py:20
  257.7 32.3 %copy-start.4 = (f32[2,128,128]{2,1,0:T(8,128)}, f32[2,128,128]{2,1,0:T(8,128)S(1)}, u32[]{:S(2)}) copy-start(f32[2,128,128]{2,1,0:T(8,128)S(1)} %fusion.60) | copy-start | bytes 393220
  257.7 3.2 collective-permute-start.20
  259.0 5.7 collective-permute-start.21
  264.7 11.1 %collective-permute-start.22 = (f32[2,384,128]{2,1,0:T(8,128)S(1)}, f32[2,384,128]{2,1,0:T(8,128)S(1)}, u32[]{:S(2)}, u32[]{:S(2)}) collective-permute-start(f32[2,384,128]{2,1,0:T(8,128)S(1)} %pad_maximum_fusion.10), channel_id=1, source_target_pairs={{0,1},{1,2},{2,3},{3,4},{4,5},{5,6},{6,7},{7,8},{8,9},{9,10},{10,1... | collective-permute-start | bytes 1179656 | tf_op jit(solution)/shard_map/ppermute | solution.py:31
  270.6 18.6 %collective-permute-start.23 = (f32[2,384,128]{2,1,0:T(8,128)S(1)}, f32[2,384,128]{2,1,0:T(8,128)S(1)}, u32[]{:S(2)}, u32[]{:S(2)}) collective-permute-start(f32[2,384,128]{2,1,0:T(8,128)S(1)} %pad_maximum_fusion.10), channel_id=1, source_target_pairs={{1,0},{2,1},{3,2},{4,3},{5,4},{6,5},{7,6},{8,7},{9,8},{10,9},{11,1... | collective-permute-start | bytes 1179656 | tf_op jit(solution)/shard_map/ppermute | solution.py:33
  290.0 0.9 copy-start.18
  290.0 1.0 copy-start.27
  290.0 1.0 copy-start.30
  294.9 0.9 copy-start.21
  294.9 1.0 copy-start.24
  312.0 7.2 %copy-start.3 = (f32[1,4,256,256]{3,1,2,0:T(4,128)S(1)}, f32[1,4,256,256]{3,1,2,0:T(4,128)}, u32[]{:S(2)}) copy-start(f32[1,4,256,256]{3,1,2,0:T(4,128)} %copy.86) | copy-start | bytes 3145732
  313.0 10.2 %collective-permute-start.24 = (f32[2,128,384]{2,1,0:T(8,128)}, f32[2,128,384]{2,1,0:T(8,128)}, u32[]{:S(2)}, u32[]{:S(2)}) collective-permute-start(f32[2,128,384]{2,1,0:T(8,128)} %get-tuple-element.349), channel_id=1, source_target_pairs={{16,0},{32,16},{48,32},{64,48},{80,64},{96,80},{112,96},{128,112},... | collective-permute-start | bytes 1179656 | tf_op jit(solution)/shard_map/ppermute | solution.py:20
  314.3 9.0 %collective-permute-start.25 = (f32[2,128,384]{2,1,0:T(8,128)}, f32[2,128,384]{2,1,0:T(8,128)}, u32[]{:S(2)}, u32[]{:S(2)}) collective-permute-start(f32[2,128,384]{2,1,0:T(8,128)} %get-tuple-element.350), channel_id=1, source_target_pairs={{0,16},{16,32},{32,48},{48,64},{64,80},{80,96},{96,112},{112,128},... | collective-permute-start | bytes 1179656 | tf_op jit(solution)/shard_map/ppermute | solution.py:20
  324.5 9.3 %collective-permute-start.26 = (f32[2,128,128]{2,1,0:T(8,128)S(1)}, f32[2,128,128]{2,1,0:T(8,128)S(1)}, u32[]{:S(2)}, u32[]{:S(2)}) collective-permute-start(f32[2,128,128]{2,1,0:T(8,128)S(1)} %get-tuple-element.364), channel_id=1, source_target_pairs={{1,0},{2,1},{3,2},{4,3},{5,4},{6,5},{7,6},{8,7},{9,8},{10,9},{11,1... | collective-permute-start | bytes 393224 | tf_op jit(solution)/shard_map/ppermute | solution.py:20
  326.4 7.4 %collective-permute-start.27 = (f32[2,128,128]{2,1,0:T(8,128)S(1)}, f32[2,128,128]{2,1,0:T(8,128)S(1)}, u32[]{:S(2)}, u32[]{:S(2)}) collective-permute-start(f32[2,128,128]{2,1,0:T(8,128)S(1)} %get-tuple-element.365), channel_id=1, source_target_pairs={{0,1},{1,2},{2,3},{3,4},{4,5},{5,6},{6,7},{7,8},{8,9},{9,10},{10,1... | collective-permute-start | bytes 393224 | tf_op jit(solution)/shard_map/ppermute | solution.py:20
  331.5 2.4 copy-start.5
  331.5 2.4 copy-start.13
Sparse Core Ops, SparseCore 0:
  323.3 277.6 all-reduce.1
where the time goes:
time: 625 us; the launch traced here: 618 us
  waiting for transfers between devices  317 us (51%)
  blocking collectives  89.7 us (14%)
  starting transfers between devices  81.5 us (13%)
  local copies, waits for them, and re-layouts  50.3 us (8%)
  other arithmetic  38.7 us (6%)
  matrix products  23.7 us (4%)
  between operations  17.9 us (3%)
    psum x1, waiting for transfers between devices, local(): summed = lax.psum(terms, ('row', 'col'))  266 us
    pmax x1, blocking collectives, local(): peak = lax.pmax(jnp.max(light), ('row', 'col'))  89.7 us
    ppermute x16, starting transfers between devices, passed_along(): return lax.ppermute(array, axis, pairs)  49.3 us
    ppermute x6, waiting for transfers between devices, with_halo(): lax.ppermute(head, axis, [((i + 1) % count, i) for i in range(ends)])  30.2 us
    dynamic_update_slice x4, local copies, waits for them, and re-layouts, place(): return lax.dynamic_update_slice(buffer, piece, start)  24.4 us
    ppermute x6, starting transfers between devices, with_halo(): lax.ppermute(tail, axis, [(i, (i + 1) % count) for i in range(ends)])  22.5 us
    unnamed x72, local copies, waits for them, and re-layouts  13.4 us
  transfers between devices with their start and end apart: 29, of which 17 were waited for; matrix products, arithmetic and copies ran while one was open for 6% of the time, Pallas kernels for 0%

commit v1 on v0

v1 whole, which is shorter than its diff:
```python
import functools
import math

import jax
import jax.numpy as jnp
import numpy as np
from jax import lax
from jax.experimental import pallas as pl
from jax.experimental.pallas import tpu as pltpu
from jax.sharding import PartitionSpec as P

ITERS = 3
W = 256
H = 128
Q = 64
MODES = 4

amp_floor = 0.25
light_ratio = 0.1
mass_ratio = 0.1
probe_step = 6.0

MESH = pl.DeviceIdType.MESH
f32 = jnp.float32
bf16 = jnp.bfloat16


def make_pairs():
    index = np.arange(W)
    turns = (index[:, None] * index[None, :]) % W
    angle = turns.astype(np.float64) * (2.0 * math.pi / W)
    real = np.cos(angle) / math.sqrt(W)
    imag = -np.sin(angle) / math.sqrt(W)
    right = np.block([[real, imag], [-imag, real]])
    left = np.block([[real, -imag], [imag, real]])
    return (right.astype(np.float32).astype(bf16), left.astype(np.float32).astype(bf16))


class Sems:
    def __init__(self):
        self.count = 0

    def take(self, n):
        first = self.count
        self.count += n
        return first


def layout(n_row, n_col):
    ny = n_col // 4
    nz = n_row // 2
    nd = 2 + int(math.log2(ny))
    sems = Sems()
    at = {}
    at["pos_r"] = sems.take(2)
    at["pos_c"] = sems.take(2)
    at["halo_r"] = sems.take(2)
    at["halo_o"] = sems.take(2)
    at["halo_s"] = sems.take(2)
    at["fold_a"] = sems.take(2)
    at["fold_b"] = sems.take(2)
    at["fold_r"] = sems.take(2)
    small = 1 + 3 + (ny - 1) + (nz - 1)
    at["small"] = [sems.take(small), sems.take(small)]
    at["rs_core"] = sems.take(4)
    at["rs_xy"] = sems.take(4 * nd)
    at["rs_z"] = sems.take(8 * nz)
    at["ag_z"] = sems.take(8 * nz)
    at["ag_xy"] = sems.take(4 * nd)
    at["ag_core"] = sems.take(4)
    return ny, nz, nd, small, at, sems.count


def kernel(
    n_row,
    n_col,
    pos_ref,
    ore_ref,
    oim_ref,
    pre_ref,
    pim_ref,
    amp_ref,
    m1_ref,
    m2_ref,
    out_re,
    out_im,
    out_p,
    tile,
    probe,
    prot,
    amps,
    m1,
    m2,
    win,
    grad,
    psi,
    hs,
    spec,
    hv,
    hh,
    sh,
    fs,
    fr,
    us,
    ur,
    light,
    posb,
    padded,
    padded64,
    sm_send,
    sm_recv,
    w_own,
    w_sib,
    r_core,
    r_xy,
    r_z,
    af,
    load_sem,
    send_sem,
    recv_sem,
):
    ny, nz, nd, n_small, at, _ = layout(n_row, n_col)
    row = lax.axis_index("row")
    col = lax.axis_index("col")
    core = lax.rem(col, 2)
    x_lo = lax.rem(col // 2, 2)
    y = col // 4
    z = lax.rem(row, nz)
    x_hi = row // nz

    def dev_at(new_x_hi, new_z, new_y, new_x_lo, new_core):
        return (new_x_hi * nz + new_z, new_y * 4 + new_x_lo * 2 + new_core)

    y0, y1 = lax.rem(y, 2), y // 2
    sibling = dev_at(x_hi, z, y, x_lo, 1 - core)
    x_1 = dev_at(x_hi, z, y, 1 - x_lo, core)
    x_2 = dev_at(1 - x_hi, z, y, x_lo, core)
    x_3 = dev_at(1 - x_hi, z, y, 1 - x_lo, core)
    y_1 = dev_at(x_hi, z, 2 * y1 + 1 - y0, x_lo, core)
    y_2 = dev_at(x_hi, z, 2 * (1 - y1) + y0, x_lo, core)
    y_3 = dev_at(x_hi, z, 2 * (1 - y1) + 1 - y0, x_lo, core)
    z_at = [lax.rem(z + k, nz) for k in range(nz)]
    z_dev = [dev_at(x_hi, z_at[k], y, x_lo, core) for k in range(nz)]
    cube = [x_1, x_3] + ([y_1, y_3] if ny == 4 else [])
    bits = [lax.rem(x_lo + x_hi, 2), x_hi] + ([lax.rem(y0 + y1, 2), y1] if ny == 4 else [])

    has = {
        "v": [row > 0, row < n_row - 1],
        "h": [col > 0, col < n_col - 1],
    }
    near = {
        "v": [(jnp.maximum(row - 1, 0), col), (jnp.minimum(row + 1, n_row - 1), col)],
        "h": [(row, jnp.maximum(col - 1, 0)), (row, jnp.minimum(col + 1, n_col - 1))],
    }

    def remote(src, dst, index_send, index_recv, dev):
        return pltpu.make_async_remote_copy(
            src_ref=src,
            dst_ref=dst,
            send_sem=send_sem.at[index_send],
            recv_sem=recv_sem.at[index_recv],
            device_id=dev,
            device_id_type=MESH,
        )

    class Pair:
        def __init__(self, axis, srcs, dst_of, first):
            self.axis = axis
            self.copies = [
                remote(srcs[d], dst_of(1 - d), first + d, first + 1 - d, near[axis][d])
                for d in range(2)
            ]

        def start(self, d=None):
            for side in (0, 1) if d is None else (d,):
                pl.when(has[self.axis][side])(self.copies[side].start)

        def recv(self, d=None):
            for side in (0, 1) if d is None else (d,):
                pl.when(has[self.axis][side])(self.copies[1 - side].wait_recv)

        def sent(self):
            for side in (0, 1):
                pl.when(has[self.axis][side])(self.copies[side].wait_send)

    loads = [
        pltpu.make_async_copy(ore_ref, tile.at[0], load_sem.at[0]),
        pltpu.make_async_copy(oim_ref, tile.at[1], load_sem.at[1]),
        pltpu.make_async_copy(pre_ref, probe.at[pl.ds(0, MODES)], load_sem.at[2]),
        pltpu.make_async_copy(pim_ref, probe.at[pl.ds(MODES, MODES)], load_sem.at[3]),
        pltpu.make_async_copy(m1_ref, m1, load_sem.at[4]),
        pltpu.make_async_copy(m2_ref, m2, load_sem.at[5]),
        pltpu.make_async_copy(amp_ref, amps, load_sem.at[6]),
    ]
    for load in loads:
        load.start()

    a_r = (pos_ref[0, 0] - (row * H - H)) // Q
    a_c = (pos_ref[0, 1] - (col * H - H)) // Q
    lr = a_r * Q
    lc = a_c * Q

    hv[...] = jnp.zeros_like(hv)
    hh[...] = jnp.zeros_like(hh)
    fr[...] = jnp.zeros_like(fr)
    ur[...] = jnp.zeros_like(ur)
    for dj in range(3):
        for di in range(3):
            posb[dj, di] = jnp.full((8, 128), 4 * di + dj, jnp.int32)
    posb[1, 1] = jnp.broadcast_to(4 * a_r + a_c, (8, 128)).astype(jnp.int32)

    barrier = pltpu.get_barrier_semaphore()
    always = [sibling, x_1, x_2, x_3] + ([y_1, y_2, y_3] if ny == 4 else []) + z_dev[1:]
    for dev in always:
        pl.semaphore_signal(barrier, inc=1, device_id=dev, device_id_type=MESH)
    expected = len(always)
    for axis in ("v", "h"):
        for d in range(2):

            def greet(axis=axis, d=d):
                pl.semaphore_signal(barrier, inc=1, device_id=near[axis][d], device_id_type=MESH)

            pl.when(has[axis][d])(greet)
            expected = expected + has[axis][d].astype(jnp.int32)
    pl.semaphore_wait(barrier, expected)

    rows_i = lax.broadcasted_iota(jnp.int32, (H, H), 0)
    cols_i = lax.broadcasted_iota(jnp.int32, (H, H), 1)
    below = rows_i < lr
    right_of = cols_i < lc

    pos_r = Pair("v", [posb.at[1, 1]] * 2, lambda d: posb.at[1, 2 * d], at["pos_r"])
    pos_c = Pair("h", [posb.at[1]] * 2, lambda d: posb.at[2 * d], at["pos_c"])
    halo_r = Pair("v", [tile] * 2, lambda d: hv.at[d], at["halo_r"])
    halo_o = Pair("h", [tile] * 2, lambda d: hh.at[d, 1], at["halo_o"])
    halo_s = Pair("h", [sh.at[0], sh.at[1]], lambda d: hh.at[d, 0], at["halo_s"])
    fold_a = Pair("h", [fs.at[0, 0], fs.at[1, 0]], lambda d: fr.at[d, 0], at["fold_a"])
    fold_b = Pair("h", [fs.at[0, 1], fs.at[1, 1]], lambda d: fr.at[d, 1], at["fold_b"])
    fold_r = Pair("v", [us.at[0], us.at[1]], lambda d: ur.at[d], at["fold_r"])

    def near_lr(d):
        return (posb[2 * d, 1][0:1, :] // 4) * Q

    groups = [[sibling], [x_1, x_2, x_3]]
    if ny == 4:
        groups.append([y_1, y_2, y_3])
    groups.append(z_dev[1:])
    small_first = [0]
    for group in groups:
        small_first.append(small_first[-1] + len(group))

    def small_copy(which, g, k):
        index = at["small"][which] + small_first[g] + k
        return remote(
            sm_send.at[which, g],
            sm_recv.at[which, small_first[g] + k],
            index,
            index,
            groups[g][k],
        )

    def small_start(which, g, value):
        sm_send[which, g] = value
        for k in range(len(groups[g])):
            small_copy(which, g, k).start()

    def small_finish(which, g, op):
        value = sm_send[which, g]
        for k in range(len(groups[g])):
            small_copy(which, g, k).wait_recv()
            value = op(value, sm_recv[which, small_first[g] + k])
        for k in range(len(groups[g])):
            small_copy(which, g, k).wait_send()
        return value

    def small_stages(which, op):
        steps = []
        for g in range(len(groups) - 1):

            def step(g=g):
                small_start(which, g + 1, small_finish(which, g, op))

            steps.append(step)
        return steps

    def halo_start():
        halo_r.start()
        halo_o.start()

    def halo_finish():
        halo_r.recv()
        for d in range(2):
            pick = rows_i < near_lr(d)
            for c in range(2):
                sh[d, c] = jnp.where(pick, hv[1, c], hv[0, c])
            halo_s.start(d)
        for c in range(2):
            win[c, H:, H:] = tile[c]
            win[c, :H, H:] = jnp.where(below, hv[1, c], hv[0, c])
        halo_o.recv()
        for c in range(2):
            win[c, H:, :H] = jnp.where(right_of, hh[1, 1, c], hh[0, 1, c])
        halo_s.recv()
        for c in range(2):
            win[c, :H, :H] = jnp.where(right_of, hh[1, 0, c], hh[0, 0, c])
        halo_r.sent()
        halo_o.sent()
        halo_s.sent()

    def product_right(table):
        for part in range(2):
            out = jnp.dot(
                psi[...], table[:, part * W : (part + 1) * W], preferred_element_type=f32
            ).astype(bf16)
            for m in range(MODES):
                hs[m, part * W : (part + 1) * W] = out[m * W : (m + 1) * W]

    def product_left(table):
        for m in range(MODES):
            spec[m] = jnp.dot(table[...], hs[m], preferred_element_type=f32)

    step_rows = 32

    def make_psi():
        def body(i, carry):
            at_row = pl.multiple_of(i * step_rows, step_rows)
            here = pl.ds(at_row, step_rows)
            wr, wi = win[0, here, :], win[1, here, :]
            for m in range(MODES):
                pr, pi = prot[m, here, :], prot[MODES + m, here, :]
                there = pl.ds(pl.multiple_of(m * W + at_row, step_rows), step_rows)
                psi[there, 0:W] = (pr * wr - pi * wi).astype(bf16)
                psi[there, W:] = (pr * wi + pi * wr).astype(bf16)
            return carry

        lax.fori_loop(0, W // step_rows, body, 0)

    def make_change():
        def body(i, carry):
            at_row = pl.multiple_of(i * step_rows, step_rows)
            here = pl.ds(at_row, step_rows)
            here_im = pl.ds(pl.multiple_of(W + at_row, step_rows), step_rows)
            total = jnp.zeros((step_rows, W), f32)
            for m in range(MODES):
                re, im = spec[m, here, :], spec[m, here_im, :]
                total = total + (re * re + im * im)
            factor = amps[here, :] * lax.rsqrt(jnp.maximum(total, amp_floor * amp_floor)) - 1.0
            for m in range(MODES):
                there = pl.ds(pl.multiple_of(m * W + at_row, step_rows), step_rows)
                psi[there, 0:W] = (spec[m, here, :] * factor).astype(bf16)
                psi[there, W:] = (spec[m, here_im, :] * factor).astype(bf16)
            return carry

        lax.fori_loop(0, W // step_rows, body, 0)

    def make_grad():
        def body(i, carry):
            at_row = pl.multiple_of(i * step_rows, step_rows)
            here = pl.ds(at_row, step_rows)
            here_im = pl.ds(pl.multiple_of(W + at_row, step_rows), step_rows)
            g_re = jnp.zeros((step_rows, W), f32)
            g_im = jnp.zeros((step_rows, W), f32)
            for m in range(MODES):
                pr, pi = prot[m, here, :], prot[MODES + m, here, :]
                er, ei = spec[m, here, :], spec[m, here_im, :]
                g_re = g_re + (pr * er + pi * ei)
                g_im = g_im + (pr * ei - pi * er)
            grad[0, here, :] = g_re
            grad[1, here, :] = g_im
            return carry

        lax.fori_loop(0, W // step_rows, body, 0)

    def fold_start():
        zero = jnp.zeros((H, H), f32)
        for part in range(2):
            half = slice(0, H) if part == 0 else slice(H, W)
            for c in range(2):
                g = grad[c, half, :H]
                fs[0, part, c] = jnp.where(right_of, zero, g)
                fs[1, part, c] = jnp.where(right_of, g, zero)
            (fold_a, fold_b)[part].start()

    def fold_middle():
        fold_a.recv()
        zero = jnp.zeros((H, H), f32)
        picks = [below, rows_i < near_lr(0), rows_i < near_lr(1)]
        for c in range(2):
            parts = [grad[c, :H, H:], fr[0, 0, c], fr[1, 0, c]]
            up, down = zero, zero
            for pick, part in zip(picks, parts):
                up = up + jnp.where(pick, zero, part)
                down = down + jnp.where(pick, part, zero)
            us[0, c] = up
            us[1, c] = down
        fold_r.start()

    def fold_finish(denom):
        fold_b.recv()
        fold_r.recv()
        for c in range(2):
            total = grad[c, H:, H:] + fr[0, 1, c] + fr[1, 1, c] + ur[0, c] + ur[1, c]
            tile[c] = tile[c] + total / denom
        fold_a.sent()
        fold_b.sent()
        fold_r.sent()

    loads[0].wait()
    loads[1].wait()
    pos_r.start()
    halo_start()
    loads[2].wait()
    loads[3].wait()

    def turned(three, back):
        rows_by = jnp.broadcast_to(a_r, three[0].shape)
        x = jnp.where(rows_by == 0, three[0], jnp.where(rows_by == 1, three[1], three[2]))
        one = pltpu.roll(x, W - Q if back else Q, 1)
        two = pltpu.roll(x, H, 1)
        cols_by = jnp.broadcast_to(a_c, x.shape)
        return jnp.where(cols_by == 0, x, jnp.where(cols_by == 1, one, two))

    def block(b):
        return slice((b % 4) * Q, (b % 4) * Q + Q)

    for b in range(4):

        def rotate(m, carry, b=b):
            prot[m, block(b), :] = turned([probe[m, block(b - t), :] for t in range(3)], False)
            return carry

        lax.fori_loop(0, 2 * MODES, rotate, 0)

    padded[...] = jnp.zeros_like(padded)
    for b in range(4):
        rows = slice(b * Q, (b + 1) * Q)
        power = jnp.zeros((Q, W), f32)
        for m in range(MODES):
            power = power + (
                probe[m, rows, :] * probe[m, rows, :]
                + probe[MODES + m, rows, :] * probe[MODES + m, rows, :]
            )
        padded[H + b * Q : H + (b + 1) * Q, H : H + W] = power
    for b in range(8):
        rows = slice(b * Q, (b + 1) * Q)
        padded64[rows, :] = pltpu.roll(padded[rows, :], Q, 1)

    pos_r.recv()
    pos_c.start()
    for load in loads[4:]:
        load.wait()
    pos_c.recv()
    pos_r.sent()
    pos_c.sent()

    peak = jnp.full((8, H), 0.0, f32)
    chunk = 32
    for r in range(H // chunk):
        total = jnp.zeros((chunk, H), f32)
        for dj in (-1, 0, 1):
            for di in (-1, 0, 1):
                code = jnp.broadcast_to(posb[dj + 1, di + 1][0:1, :], (chunk, H))
                part = jnp.zeros((chunk, H), f32)
                for ar in range(3):
                    if (di, ar) in ((-1, 0), (1, 2)):
                        continue
                    from_row = H + H * (1 - di) - Q * ar + r * chunk
                    for ac in range(3):
                        if (dj, ac) in ((-1, 0), (1, 2)):
                            continue
                        from_col = H + H * (1 - dj) - Q * ac
                        if ac == 1:
                            piece = padded64[
                                from_row : from_row + chunk, from_col + Q : from_col + Q + H
                            ]
                        else:
                            piece = padded[from_row : from_row + chunk, from_col : from_col + H]
                        part = jnp.where(code == 4 * ar + ac, piece, part)
                total = total + part
        light[r * chunk : (r + 1) * chunk, :] = total
        for k in range(chunk // 8):
            peak = jnp.maximum(peak, total[k * 8 : (k + 1) * 8, :])
    small_start(0, 0, peak)

    def one_pass(hooks):
        hooks = list(hooks)

        def hook():
            if hooks:
                hooks.pop(0)()

        make_psi()
        product_right(m1)
        hook()
        product_left(m2)
        hook()
        make_change()
        product_right(m2)
        hook()
        product_left(m1)
        hook()
        make_grad()

    def peak_of():
        value = small_finish(0, len(groups) - 1, jnp.maximum)
        light[...] = light[...] + light_ratio * jnp.max(value)

    halo_finish()
    one_pass(small_stages(0, jnp.maximum))
    fold_start()
    fold_middle()
    peak_of()
    fold_finish(light[...])

    halo_start()
    halo_finish()
    one_pass([])
    fold_start()
    fold_middle()
    fold_finish(light[...])

    halo_start()
    halo_finish()
    mass = jnp.zeros((8, W), f32)
    for r in range(W // 8):
        wr, wi = win[0, r * 8 : (r + 1) * 8, :], win[1, r * 8 : (r + 1) * 8, :]
        mass = mass + (wr * wr + wi * wi)
    small_start(1, 0, mass[:, :H] + mass[:, H:])
    one_pass(small_stages(1, jnp.add))
    fold_start()

    sib = 1 - core

    def put(target, k, comp, value):
        for lh in range(2):
            target[k, lh * 8 : (lh + 1) * 8, comp] = value[:, lh * H : (lh + 1) * H].reshape(
                8, 8, H
            )

    rs_core = [
        remote(w_sib.at[k], r_core.at[k], at["rs_core"] + k, at["rs_core"] + k, sibling)
        for k in range(4)
    ]

    def mode_products(m, carry):
        for b in range(4):
            here = block(b)
            here_im = slice(W + b * Q, W + b * Q + Q)
            wr, wi = win[0, here, :], win[1, here, :]
            er, ei = spec[m, here, :], spec[m, here_im, :]
            spec[m, here, :] = wr * er + wi * ei
            spec[m, here_im, :] = wr * ei - wi * er
        return carry

    lax.fori_loop(0, MODES, mode_products, 0)
    for b in range(4):
        wr, wi = win[0, block(b), :], win[1, block(b), :]
        win[0, block(b), :] = wr * wr + wi * wi

    def mode_grad(k, m):
        return (
            turned([spec[m, block(k + t), :] for t in range(3)], True),
            turned(
                [spec[m, pl.ds(W + ((k + t) % 4) * Q, Q), :] for t in range(3)], True
            ),
        )

    for k in range(4):
        mass_k = turned([win[0, block(k + t), :] for t in range(3)], True)
        put(w_sib, k, 2, mass_k)
        put(w_own, k, 2, mass_k)
        for mm in range(2):
            g_re, g_im = mode_grad(k, 2 * sib + mm)
            put(w_sib, k, 3 * mm, g_re)
            put(w_sib, k, 3 * mm + 1, g_im)
        rs_core[k].start()
    for k in range(4):
        for mm in range(2):
            g_re, g_im = mode_grad(k, 2 * core + mm)
            put(w_own, k, 3 * mm, g_re)
            put(w_own, k, 3 * mm + 1, g_im)
    fold_middle()

    base = []
    bases = []
    for k in range(4):
        rs_core[k].wait_recv()

        def add_core(b, carry, k=k):
            w_own[k, b] = w_own[k, b] + r_core[k, b]
            return carry

        lax.fori_loop(0, 16, add_core, 0, unroll=4)
        base.append(0)
        bases.append([])
    offsets = [0, 8, 12, 14]

    def rs_copy(k, s):
        d = (k + s) % nd
        size = 8 >> s
        give = base[k] + (1 - bits[d]) * size
        index = at["rs_xy"] + k * nd + s
        return remote(
            w_own.at[k, pl.ds(give, size)],
            r_xy.at[k, pl.ds(offsets[s], size)],
            index,
            index,
            cube[d],
        )

    for s in range(nd):
        copies = [rs_copy(k, s) for k in range(4)]
        for copy in copies:
            copy.start()
        if s == 1:
            fold_finish(light[...])
        size = 8 >> s
        for k in range(4):
            copies[k].wait_recv()
            bases[k].append(base[k])
            keep = base[k] + bits[(k + s) % nd] * size
            for b in range(size):
                w_own[k, keep + b] = w_own[k, keep + b] + r_xy[k, offsets[s] + b]
            base[k] = keep
        for copy in copies:
            copy.wait_send()
    for k in range(4):
        rs_core[k].wait_send()
    save = [
        pltpu.make_async_copy(tile.at[0], out_re, load_sem.at[0]),
        pltpu.make_async_copy(tile.at[1], out_im, load_sem.at[1]),
    ]
    for copy in save:
        copy.start()

    left = 16 >> nd
    per = 8 // nz

    def part_of(slot):
        return slot // 2, lax.rem(slot, 2)

    def base_of(part):
        value = base[0] * 0
        for k in range(4):
            value = value + (part == k).astype(jnp.int32) * base[k]
        return value

    def z_copy(k, q):
        part, mode = part_of(z_at[k] * per + q)
        index = at["rs_z"] + k * per + q
        return remote(
            w_own.at[part, pl.ds(base_of(part), left), pl.ds(2 * mode, 3)],
            r_z.at[k, q],
            index,
            index,
            z_dev[k],
        )

    def z_back(k, q):
        part, mode = part_of(z * per + q)
        where = af.at[core, part, pl.ds(base_of(part), left), mode]
        index = at["ag_z"] + k * per + q
        return remote(where, where, index, index, z_dev[k])

    def z_back_recv(k, q):
        part, mode = part_of(lax.rem(z + nz - k, nz) * per + q)
        where = af.at[core, part, pl.ds(base_of(part), left), mode]
        index = at["ag_z"] + k * per + q
        return remote(where, where, index, index, z_dev[k])

    for k in range(1, nz):
        for q in range(per):
            z_copy(k, q).start()
    mass_sum = small_finish(1, len(groups) - 1, jnp.add)
    mean_mass = jnp.sum(mass_sum) / (W * W)
    for q in range(per):
        part, mode = part_of(z * per + q)
        first = base_of(part)
        sums = []
        for b in range(left):
            sums.append([w_own[part, first + b, 2 * mode + e] for e in range(3)])
        for k in range(1, nz):
            z_copy(k, q).wait_recv()
            for b in range(left):
                for e in range(3):
                    sums[b][e] = sums[b][e] + r_z[k, q, b, e]
        for b in range(left):
            spot = first + b
            at_row = pl.multiple_of(part * Q + lax.rem(spot, 8) * 8, 8)
            at_col = pl.multiple_of((spot // 8) * H, H)
            first_is_re = jnp.broadcast_to(mode, (8, H)) == 0
            mass_here = jnp.where(first_is_re, sums[b][2], sums[b][0])
            g_re = jnp.where(first_is_re, sums[b][0], sums[b][1])
            g_im = jnp.where(first_is_re, sums[b][1], sums[b][2])
            scale = probe_step / (mass_here + mass_ratio * mean_mass)
            m = 2 * core + mode
            old_re = probe[m, pl.ds(at_row, 8), pl.ds(at_col, H)]
            old_im = probe[MODES + m, pl.ds(at_row, 8), pl.ds(at_col, H)]
            af[core, part, spot, mode, 0] = old_re + g_re * scale
            af[core, part, spot, mode, 1] = old_im + g_im * scale
        for k in range(1, nz):
            z_back(k, q).start()
    for k in range(1, nz):
        for q in range(per):
            z_copy(k, q).wait_send()
            z_back_recv(k, q).wait_recv()

    def ag_copy(k, s):
        d = (k + s) % nd
        size = 8 >> s
        mine = bases[k][s] + bits[d] * size
        where = af.at[core, k, pl.ds(mine, size)]
        index = at["ag_xy"] + k * nd + s
        return remote(where, where, index, index, cube[d])

    def ag_recv(k, s):
        d = (k + s) % nd
        size = 8 >> s
        other = bases[k][s] + (1 - bits[d]) * size
        where = af.at[core, k, pl.ds(other, size)]
        index = at["ag_xy"] + k * nd + s
        return remote(where, where, index, index, cube[d])

    def ag_core(k, which):
        where = af.at[which, k]
        index = at["ag_core"] + k
        return remote(where, where, index, index, sibling)

    for s in reversed(range(nd)):
        for k in range(4):
            ag_copy(k, s).start()
        for k in range(4):
            ag_recv(k, s).wait_recv()
            if s == 0:
                ag_core(k, core).start()
    for k in range(4):
        ag_core(k, sib).wait_recv()
    save.append(pltpu.make_async_copy(af, out_p, load_sem.at[2]))
    save[-1].start()
    for k in range(1, nz):
        for q in range(per):
            z_back(k, q).wait_send()
    for s in range(nd):
        for k in range(4):
            ag_copy(k, s).wait_send()
    for k in range(4):
        ag_core(k, core).wait_send()
    for copy in save:
        copy.wait()


def local(n_row, n_col, obj_re, obj_im, probe_re, probe_im, amps, positions):
    ny, nz, nd, n_small, at, n_sems = layout(n_row, n_col)
    right, left = make_pairs()
    any_spec = pl.BlockSpec(memory_space=pl.ANY)
    n_groups = 4 if ny == 4 else 3
    keep = 16 >> nd
    per = 8 // nz
    out_re, out_im, out_p = pl.pallas_call(
        functools.partial(kernel, n_row, n_col),
        out_shape=(
            jax.ShapeDtypeStruct((H, H), f32),
            jax.ShapeDtypeStruct((H, H), f32),
            jax.ShapeDtypeStruct((2, 4, 16, 2, 2, 8, H), f32),
        ),
        in_specs=[pl.BlockSpec(memory_space=pltpu.SMEM)] + [any_spec] * 7,
        out_specs=(any_spec, any_spec, any_spec),
        scratch_shapes=[
            pltpu.VMEM((2, H, H), f32),
            pltpu.VMEM((2 * MODES, W, W), f32),
            pltpu.VMEM((2 * MODES, W, W), f32),
            pltpu.VMEM((W, W), f32),
            pltpu.VMEM((2 * W, 2 * W), bf16),
            pltpu.VMEM((2 * W, 2 * W), bf16),
            pltpu.VMEM((2, W, W), f32),
            pltpu.VMEM((2, W, W), f32),
            pltpu.VMEM((MODES * W, 2 * W), bf16),
            pltpu.VMEM((MODES, 2 * W, W), bf16),
            pltpu.VMEM((MODES, 2 * W, W), f32),
            pltpu.VMEM((2, 2, H, H), f32),
            pltpu.VMEM((2, 2, 2, H, H), f32),
            pltpu.VMEM((2, 2, H, H), f32),
            pltpu.VMEM((2, 2, 2, H, H), f32),
            pltpu.VMEM((2, 2, 2, H, H), f32),
            pltpu.VMEM((2, 2, H, H), f32),
            pltpu.VMEM((2, 2, H, H), f32),
            pltpu.VMEM((H, H), f32),
            pltpu.VMEM((3, 3, 8, H), jnp.int32),
            pltpu.VMEM((2 * W, 2 * W), f32),
            pltpu.VMEM((2 * W, 2 * W), f32),
            pltpu.VMEM((2, n_groups, 8, H), f32),
            pltpu.VMEM((2, n_small, 8, H), f32),
            pltpu.VMEM((4, 16, 5, 8, H), f32),
            pltpu.VMEM((4, 16, 5, 8, H), f32),
            pltpu.VMEM((4, 16, 5, 8, H), f32),
            pltpu.VMEM((4, 15, 5, 8, H), f32),
            pltpu.VMEM((nz, per, keep, 3, 8, H), f32),
            pltpu.VMEM((2, 4, 16, 2, 2, 8, H), f32),
            pltpu.SemaphoreType.DMA((7,)),
            pltpu.SemaphoreType.DMA((n_sems,)),
            pltpu.SemaphoreType.DMA((n_sems,)),
        ],
        compiler_params=pltpu.CompilerParams(
            collective_id=0, has_side_effects=True, vmem_limit_bytes=48 << 20
        ),
    )(
        positions.reshape(1, 2),
        obj_re,
        obj_im,
        probe_re,
        probe_im,
        amps.reshape(W, W),
        jnp.asarray(right),
        jnp.asarray(left),
    )
    parts = out_p.reshape(2, 4, 2, 8, 2, 2, 8, H)
    new = parts.transpose(5, 0, 4, 1, 3, 6, 2, 7).reshape(2, MODES, W, W)
    return (out_re, out_im, new[0], new[1])


def solution(mesh):
    n_row, n_col = mesh.shape["row"], mesh.shape["col"]
    placed = (
        P("row", "col"),
        P("row", "col"),
        P(),
        P(),
        P("row", "col", None, None, None),
        P("row", "col", None, None),
    )
    return jax.shard_map(
        functools.partial(local, n_row, n_col),
        mesh=mesh,
        in_specs=placed,
        out_specs=(P("row", "col"), P("row", "col"), P(), P()),
        check_vma=False,
    )
```

time: 625 us -> 153 us (0.24)
  waiting for transfers between devices: 317 us -> 0 us
  Pallas kernels: 0 us -> 141 us
  blocking collectives: 89.7 us -> 0 us
  starting transfers between devices: 81.5 us -> 0 us
  local copies, waits for them, and re-layouts: 50.3 us -> 11.5 us
  other arithmetic: 38.7 us -> 0 us
  matrix products: 23.7 us -> 0 us
  between operations: 17.9 us -> 0.67 us
    psum x1 -> x0, waiting for transfers between devices: 266 us -> none  [local(): summed = lax.psum(terms, ('row', 'col'))]
    pallas_call x0 -> x1, Pallas kernels: none -> 141 us  [local(): pl.pallas_call(functools.partial(kernel, n_row, n_col), out_shape=(jax.Sh...]
    pmax x1 -> x0, blocking collectives: 89.7 us -> none  [local(): peak = lax.pmax(jnp.max(light), ('row', 'col'))]
    ppermute x28 -> x0, starting transfers between devices: 81.5 us -> none  [the longest x16 49.3 us: passed_along(): return lax.ppermute(array, axis, pairs)]
    ppermute x28 -> x0, waiting for transfers between devices: 50.3 us -> none  [the longest x6 30.2 us: with_halo(): lax.ppermute(head, axis, [((i + 1) % count, i) for i in range(ends)])]
    dynamic_update_slice x4 -> x0, local copies, waits for them, and re-layouts: 24.4 us -> none  [place(): return lax.dynamic_update_slice(buffer, piece, start)]
    dot_general x18 -> x0, matrix products: 23.7 us -> none  [the longest x6 9.72 us: transform(): jnp.einsum('kn,mnd->mkd', imag, half, preferred_element_type=jnp.float32)]
    concatenate x7 -> x0, other arithmetic: 8.73 us -> none  [the longest x6 4.8 us: with_halo(): jnp.concatenate([lax.ppermute(tail, axis, [(i, (i + 1) % count) for i in...]
  transfers between devices with their start and end apart: 29 -> 0, of which waited for: 17 -> 0; matrix products, arithmetic and copies ran while one was open for 6% -> 0% of each run, Pallas kernels for 0% -> 0%
where the time goes in v1:
time: 153 us
  Pallas kernels  141 us (92%)
  local copies, waits for them, and re-layouts  11.5 us (8%)
    pallas_call x1, Pallas kernels, local(): pl.pallas_call(functools.partial(kernel, n_row, n_col), out_shape=(jax.Sh...  141 us
    unnamed x18, local copies, waits for them, and re-layouts  9.06 us

profile of v1, /device:TPU:1, one launch (start us, length us, event | category | flops | bytes accessed | tf_op | source)
XLA Modules:
  0.0 152.7 jit_solution(12921524038372919149)
XLA Ops:
  0.6 0.0 copy-start
  0.6 1.2 copy-done
  1.9 0.0 copy-start.1
  1.9 1.2 copy-done.1
  3.1 0.0 copy-start.2
  3.1 1.0 copy-done.2
  4.1 0.0 copy-start.3
  4.1 1.0 copy-done.3
  5.2 0.0 copy-start.4
  5.2 0.9 copy-done.4
  6.1 0.0 copy-start.5
  6.1 0.8 copy-done.5
  7.0 0.0 copy-start.6
  7.0 0.8 copy-done.6
  7.8 0.0 copy-start.7
  7.8 0.7 copy-done.7
  8.5 140.6 %shard_map.111 = (f32[128,128]{1,0:T(8,128)S(1)}, f32[128,128]{1,0:T(8,128)S(1)}, f32[2,4,16,2,2,8,128]{6,5,4,3,2,1,0:T(8,128)S(1)}) custom-call(s32[1,2]{1,0:T(1,128)S(1)} %bitcast.9, f32[128,128]{1,0:T(8,128)S(1)} %copy-done.5, f32[128,128]{1,0:T(8,128)S(1)} %copy-done.6, f32[4,256,256]{2,1,0:T(8,128)S(1)} %copy-done, f32[4,256,256]{2,1,0:T(8,128)S(1)} %copy-done.1, ...), custom_call_target="tpu_custom_call" | custom-call | tf_op jit(solution)/shard_map/pallas_call | solution.py:759
  149.0 0.3 fusion
  149.3 1.1 copy.13
  150.4 1.1 copy.12
  151.4 0.6 copy.16
  152.1 0.6 copy.17
Async XLA Ops:
  0.6 1.2 copy-start
  1.9 1.2 copy-start.1
  3.1 1.0 copy-start.2
  4.1 1.0 copy-start.3
  5.2 0.9 copy-start.4
  6.1 0.8 copy-start.5
  7.0 0.8 copy-start.6
  7.8 0.7 copy-start.7

commit v2 on v1

--- a/solution.py
+++ b/solution.py
@@ -46,29 +46,26 @@
         return first
 
 
-def layout(n_row, n_col):
-    ny = n_col // 4
-    nz = n_row // 2
-    nd = 2 + int(math.log2(ny))
+NX, NY, NZ = 4, 4, 8
+
+
+def layout():
     sems = Sems()
     at = {}
-    at["pos_r"] = sems.take(2)
-    at["pos_c"] = sems.take(2)
-    at["halo_r"] = sems.take(2)
-    at["halo_o"] = sems.take(2)
-    at["halo_s"] = sems.take(2)
-    at["fold_a"] = sems.take(2)
-    at["fold_b"] = sems.take(2)
-    at["fold_r"] = sems.take(2)
-    small = 1 + 3 + (ny - 1) + (nz - 1)
+    for name in ("pos_r", "pos_c", "halo_r", "halo_o", "halo_s", "fold_a", "fold_b", "fold_r"):
+        at[name] = sems.take(2)
+    small = 1 + 3 + 3 + 7
     at["small"] = [sems.take(small), sems.take(small)]
+    at["mass"] = sems.take(small + 1)
     at["rs_core"] = sems.take(4)
-    at["rs_xy"] = sems.take(4 * nd)
-    at["rs_z"] = sems.take(8 * nz)
-    at["ag_z"] = sems.take(8 * nz)
-    at["ag_xy"] = sems.take(4 * nd)
+    at["rs_f"] = sems.take(12)
+    at["rs_g"] = sems.take(12)
+    at["rs_z"] = sems.take(NZ)
+    at["ag_z"] = sems.take(NZ)
+    at["ag_g"] = sems.take(12)
+    at["ag_f"] = sems.take(12)
     at["ag_core"] = sems.take(4)
-    return ny, nz, nd, small, at, sems.count
+    return small, at, sems.count
 
 
 def kernel(
@@ -84,7 +81,8 @@
     m2_ref,
     out_re,
     out_im,
-    out_p,
+    out_pre,
+    out_pim,
     tile,
     probe,
     prot,
@@ -112,37 +110,52 @@
     w_own,
     w_sib,
     r_core,
-    r_xy,
+    r_f,
+    r_g,
     r_z,
+    wm,
+    rm_core,
+    rm_f,
+    rm_g,
+    rm_z,
     af,
     load_sem,
     send_sem,
     recv_sem,
 ):
-    ny, nz, nd, n_small, at, _ = layout(n_row, n_col)
+    n_small, at, _ = layout()
+    nz = NZ
     row = lax.axis_index("row")
     col = lax.axis_index("col")
     core = lax.rem(col, 2)
-    x_lo = lax.rem(col // 2, 2)
+    x = 2 * (row // nz) + lax.rem(col // 2, 2)
     y = col // 4
     z = lax.rem(row, nz)
-    x_hi = row // nz
-
-    def dev_at(new_x_hi, new_z, new_y, new_x_lo, new_core):
-        return (new_x_hi * nz + new_z, new_y * 4 + new_x_lo * 2 + new_core)
-
-    y0, y1 = lax.rem(y, 2), y // 2
-    sibling = dev_at(x_hi, z, y, x_lo, 1 - core)
-    x_1 = dev_at(x_hi, z, y, 1 - x_lo, core)
-    x_2 = dev_at(1 - x_hi, z, y, x_lo, core)
-    x_3 = dev_at(1 - x_hi, z, y, 1 - x_lo, core)
-    y_1 = dev_at(x_hi, z, 2 * y1 + 1 - y0, x_lo, core)
-    y_2 = dev_at(x_hi, z, 2 * (1 - y1) + y0, x_lo, core)
-    y_3 = dev_at(x_hi, z, 2 * (1 - y1) + 1 - y0, x_lo, core)
+
+    def dev_at(new_x, new_y, new_z, new_core):
+        return ((new_x // 2) * nz + new_z, new_y * 4 + lax.rem(new_x, 2) * 2 + new_core)
+
+    def flip(value, q):
+        low, high = lax.rem(value, 2), value // 2
+        low = 1 - low if q % 2 else low
+        high = 1 - high if q // 2 else high
+        return 2 * high + low
+
+    sibling = dev_at(x, y, z, 1 - core)
+    f = jnp.where(core == 0, x, y)
+    g = jnp.where(core == 0, y, x)
+
+    def dev_of(new_f, new_g):
+        return dev_at(
+            jnp.where(core == 0, new_f, new_g), jnp.where(core == 0, new_g, new_f), z, core
+        )
+
+    f_at = [flip(f, q) for q in range(4)]
+    g_at = [flip(g, q) for q in range(4)]
+    f_dev = [dev_of(f_at[q], g) for q in range(4)]
+    g_dev = [dev_of(f, g_at[q]) for q in range(4)]
     z_at = [lax.rem(z + k, nz) for k in range(nz)]
-    z_dev = [dev_at(x_hi, z_at[k], y, x_lo, core) for k in range(nz)]
-    cube = [x_1, x_3] + ([y_1, y_3] if ny == 4 else [])
-    bits = [lax.rem(x_lo + x_hi, 2), x_hi] + ([lax.rem(y0 + y1, 2), y1] if ny == 4 else [])
+    z_dev = [dev_at(x, y, z_at[k], core) for k in range(nz)]
 
     has = {
         "v": [row > 0, row < n_row - 1],
@@ -210,7 +223,7 @@
     posb[1, 1] = jnp.broadcast_to(4 * a_r + a_c, (8, 128)).astype(jnp.int32)
 
     barrier = pltpu.get_barrier_semaphore()
-    always = [sibling, x_1, x_2, x_3] + ([y_1, y_2, y_3] if ny == 4 else []) + z_dev[1:]
+    always = [sibling] + f_dev[1:] + g_dev[1:] + z_dev[1:]
     for dev in always:
         pl.semaphore_signal(barrier, inc=1, device_id=dev, device_id_type=MESH)
     expected = len(always)
@@ -241,10 +254,7 @@
     def near_lr(d):
         return (posb[2 * d, 1][0:1, :] // 4) * Q
 
-    groups = [[sibling], [x_1, x_2, x_3]]
-    if ny == 4:
-        groups.append([y_1, y_2, y_3])
-    groups.append(z_dev[1:])
+    groups = [[sibling], f_dev[1:], g_dev[1:], z_dev[1:]]
     small_first = [0]
     for group in groups:
         small_first.append(small_first[-1] + len(group))
@@ -273,33 +283,31 @@
             small_copy(which, g, k).wait_send()
         return value
 
-    def small_stages(which, op):
-        steps = []
-        for g in range(len(groups) - 1):
-
-            def step(g=g):
-                small_start(which, g + 1, small_finish(which, g, op))
-
-            steps.append(step)
-        return steps
+    def small_next(which, g, op):
+        small_start(which, g + 1, small_finish(which, g, op))
 
     def halo_start():
         halo_r.start()
         halo_o.start()
 
-    def halo_finish():
+    def nothing():
+        pass
+
+    def halo_finish(first=nothing, second=nothing):
         halo_r.recv()
         for d in range(2):
             pick = rows_i < near_lr(d)
             for c in range(2):
                 sh[d, c] = jnp.where(pick, hv[1, c], hv[0, c])
             halo_s.start(d)
+        first()
         for c in range(2):
             win[c, H:, H:] = tile[c]
             win[c, :H, H:] = jnp.where(below, hv[1, c], hv[0, c])
         halo_o.recv()
         for c in range(2):
             win[c, H:, :H] = jnp.where(right_of, hh[1, 1, c], hh[0, 1, c])
+        second()
         halo_s.recv()
         for c in range(2):
             win[c, :H, :H] = jnp.where(right_of, hh[1, 0, c], hh[0, 0, c])
@@ -381,7 +389,8 @@
                 fs[1, part, c] = jnp.where(right_of, g, zero)
             (fold_a, fold_b)[part].start()
 
-    def fold_middle():
+    def fold_middle(first=nothing):
+        first()
         fold_a.recv()
         zero = jnp.zeros((H, H), f32)
         picks = [below, rows_i < near_lr(0), rows_i < near_lr(1)]
@@ -453,94 +462,136 @@
     pos_r.sent()
     pos_c.sent()
 
-    peak = jnp.full((8, H), 0.0, f32)
-    chunk = 32
-    for r in range(H // chunk):
-        total = jnp.zeros((chunk, H), f32)
-        for dj in (-1, 0, 1):
-            for di in (-1, 0, 1):
-                code = jnp.broadcast_to(posb[dj + 1, di + 1][0:1, :], (chunk, H))
-                part = jnp.zeros((chunk, H), f32)
-                for ar in range(3):
-                    if (di, ar) in ((-1, 0), (1, 2)):
-                        continue
-                    from_row = H + H * (1 - di) - Q * ar + r * chunk
-                    for ac in range(3):
-                        if (dj, ac) in ((-1, 0), (1, 2)):
+    def make_light():
+        peak = jnp.full((8, H), 0.0, f32)
+        chunk = 32
+        for r in range(H // chunk):
+            total = jnp.zeros((chunk, H), f32)
+            for dj in (-1, 0, 1):
+                for di in (-1, 0, 1):
+                    code = jnp.broadcast_to(posb[dj + 1, di + 1][0:1, :], (chunk, H))
+                    part = jnp.zeros((chunk, H), f32)
+                    for ar in range(3):
+                        if (di, ar) in ((-1, 0), (1, 2)):
                             continue
-                        from_col = H + H * (1 - dj) - Q * ac
-                        if ac == 1:
-                            piece = padded64[
-                                from_row : from_row + chunk, from_col + Q : from_col + Q + H
-                            ]
-                        else:
-                            piece = padded[from_row : from_row + chunk, from_col : from_col + H]
-                        part = jnp.where(code == 4 * ar + ac, piece, part)
-                total = total + part
-        light[r * chunk : (r + 1) * chunk, :] = total
-        for k in range(chunk // 8):
-            peak = jnp.maximum(peak, total[k * 8 : (k + 1) * 8, :])
-    small_start(0, 0, peak)
-
-    def one_pass(hooks):
-        hooks = list(hooks)
-
-        def hook():
-            if hooks:
-                hooks.pop(0)()
-
+                        from_row = H + H * (1 - di) - Q * ar + r * chunk
+                        for ac in range(3):
+                            if (dj, ac) in ((-1, 0), (1, 2)):
+                                continue
+                            from_col = H + H * (1 - dj) - Q * ac
+                            if ac == 1:
+                                piece = padded64[
+                                    from_row : from_row + chunk, from_col + Q : from_col + Q + H
+                                ]
+                            else:
+                                piece = padded[from_row : from_row + chunk, from_col : from_col + H]
+                            part = jnp.where(code == 4 * ar + ac, piece, part)
+                    total = total + part
+            light[r * chunk : (r + 1) * chunk, :] = total
+            for k in range(chunk // 8):
+                peak = jnp.maximum(peak, total[k * 8 : (k + 1) * 8, :])
+        small_start(0, 0, peak)
+
+    def one_pass(first=nothing, second=nothing):
         make_psi()
         product_right(m1)
-        hook()
+        first()
         product_left(m2)
-        hook()
         make_change()
         product_right(m2)
-        hook()
+        second()
         product_left(m1)
-        hook()
         make_grad()
 
-    def peak_of():
-        value = small_finish(0, len(groups) - 1, jnp.maximum)
-        light[...] = light[...] + light_ratio * jnp.max(value)
-
-    halo_finish()
-    one_pass(small_stages(0, jnp.maximum))
+    halo_finish(make_light, lambda: small_next(0, 0, jnp.maximum))
+    one_pass(nothing, lambda: small_next(0, 1, jnp.maximum))
     fold_start()
-    fold_middle()
-    peak_of()
+    fold_middle(lambda: small_next(0, 2, jnp.maximum))
+    peak = small_finish(0, 3, jnp.maximum)
+    light[...] = light[...] + light_ratio * jnp.max(peak)
     fold_finish(light[...])
 
     halo_start()
     halo_finish()
-    one_pass([])
+    one_pass()
     fold_start()
     fold_middle()
     fold_finish(light[...])
 
     halo_start()
     halo_finish()
+    spot = 4 * f + g
+
+    def mass_copies(stage):
+        first = at["mass"] + small_first[stage]
+        if stage == 0:
+            return [remote(wm.at[0], rm_core, first, first, sibling)]
+        if stage == 1:
+            return [
+                remote(
+                    wm.at[1, :, pl.ds(4 * f_at[q], 4)], rm_f.at[q - 1], first + q, first + q, f_dev[q]
+                )
+                for q in range(1, 4)
+            ]
+        if stage == 2:
+            return [
+                remote(
+                    wm.at[1, :, pl.ds(4 * f + g_at[q], 1)],
+                    rm_g.at[q - 1],
+                    first + q,
+                    first + q,
+                    g_dev[q],
+                )
+                for q in range(1, 4)
+            ]
+        return [
+            remote(wm.at[1, z_at[k] // 2, spot], rm_z.at[k], first + k, first + k, z_dev[k])
+            for k in range(1, nz)
+        ]
+
+    def mass_next(stage):
+        for copy in mass_copies(stage):
+            copy.wait_recv()
+        if stage == 0:
+            wm[1] = wm[0] + rm_core[...]
+        elif stage == 1:
+            mine = pl.ds(4 * f, 4)
+            wm[1, :, mine] = wm[1, :, mine] + (rm_f[0] + rm_f[1] + rm_f[2])
+        elif stage == 2:
+            mine = pl.ds(spot, 1)
+            wm[1, :, mine] = wm[1, :, mine] + (rm_g[0] + rm_g[1] + rm_g[2])
+        for copy in mass_copies(stage):
+            copy.wait_send()
+        if stage < 3:
+            for copy in mass_copies(stage + 1):
+                copy.start()
+        if stage < 3:
+            small_next(1, stage, jnp.add)
+
+    def put(store, value):
+        for lh in range(2):
+            store(lh, value[:, lh * H : (lh + 1) * H].reshape(8, 8, H))
+
     mass = jnp.zeros((8, W), f32)
-    for r in range(W // 8):
-        wr, wi = win[0, r * 8 : (r + 1) * 8, :], win[1, r * 8 : (r + 1) * 8, :]
-        mass = mass + (wr * wr + wi * wi)
+    for b in range(4):
+        wr, wi = win[0, block(b), :], win[1, block(b), :]
+        here = wr * wr + wi * wi
+        grad[0, block(b), :] = here
+        for r in range(8):
+            mass = mass + here[r * 8 : (r + 1) * 8]
     small_start(1, 0, mass[:, :H] + mass[:, H:])
-    one_pass(small_stages(1, jnp.add))
+    for k in range(4):
+
+        def store_mass(lh, value, k=k):
+            wm[0, k, lh * 8 : (lh + 1) * 8] = value
+
+        put(store_mass, turned([grad[0, block(k + t), :] for t in range(3)], True))
+    mass_copies(0)[0].start()
+
+    one_pass(nothing, lambda: mass_next(0))
     fold_start()
 
     sib = 1 - core
-
-    def put(target, k, comp, value):
-        for lh in range(2):
-            target[k, lh * 8 : (lh + 1) * 8, comp] = value[:, lh * H : (lh + 1) * H].reshape(
-                8, 8, H
-            )
-
-    rs_core = [
-        remote(w_sib.at[k], r_core.at[k], at["rs_core"] + k, at["rs_core"] + k, sibling)
-        for k in range(4)
-    ]
 
     def mode_products(m, carry):
         for b in range(4):
@@ -553,37 +604,64 @@
         return carry
 
     lax.fori_loop(0, MODES, mode_products, 0)
-    for b in range(4):
-        wr, wi = win[0, block(b), :], win[1, block(b), :]
-        win[0, block(b), :] = wr * wr + wi * wi
-
-    def mode_grad(k, m):
-        return (
-            turned([spec[m, block(k + t), :] for t in range(3)], True),
-            turned(
-                [spec[m, pl.ds(W + ((k + t) % 4) * Q, Q), :] for t in range(3)], True
-            ),
+
+    def put_part(target, k, which):
+        for mm in range(2):
+            for c in range(2):
+
+                def store(lh, value, comp=2 * mm + c):
+                    target[k, lh * 8 : (lh + 1) * 8, comp] = value
+
+                put(
+                    store,
+                    turned(
+                        [
+                            spec[2 * which + mm, pl.ds(c * W + ((k + t) % 4) * Q, Q), :]
+                            for t in range(3)
+                        ],
+                        True,
+                    ),
+                )
+
+    rs_core = [
+        remote(w_sib.at[k], r_core.at[k], at["rs_core"] + k, at["rs_core"] + k, sibling)
+        for k in range(4)
+    ]
+    for k in range(4):
+        put_part(w_sib, k, sib)
+        rs_core[k].start()
+
+    def rs_f(k):
+        first = at["rs_f"] + 3 * k - 1
+        return [
+            remote(
+                w_own.at[k, pl.ds(4 * f_at[q], 4)], r_f.at[k, q - 1], first + q, first + q, f_dev[q]
+            )
+            for q in range(1, 4)
+        ]
+
+    def rs_g(k):
+        first = at["rs_g"] + 3 * k - 1
+        return [
+            remote(w_own.at[k, 4 * f + g_at[q]], r_g.at[k, q - 1], first + q, first + q, g_dev[q])
+            for q in range(1, 4)
+        ]
+
+    def rs_z(k, mode):
+        to = 2 * k + mode
+        return remote(
+            w_own.at[k, spot, pl.ds(2 * mode, 2)],
+            r_z.at[z],
+            at["rs_z"] + to,
+            at["rs_z"] + z,
+            dev_at(x, y, to, core),
         )
 
+    def rs_z_from(k):
+        return remote(r_z.at[k], r_z.at[k], at["rs_z"] + k, at["rs_z"] + k, dev_at(x, y, k, core))
+
     for k in range(4):
-        mass_k = turned([win[0, block(k + t), :] for t in range(3)], True)
-        put(w_sib, k, 2, mass_k)
-        put(w_own, k, 2, mass_k)
-        for mm in range(2):
-            g_re, g_im = mode_grad(k, 2 * sib + mm)
-            put(w_sib, k, 3 * mm, g_re)
-            put(w_sib, k, 3 * mm + 1, g_im)
-        rs_core[k].start()
-    for k in range(4):
-        for mm in range(2):
-            g_re, g_im = mode_grad(k, 2 * core + mm)
-            put(w_own, k, 3 * mm, g_re)
-            put(w_own, k, 3 * mm + 1, g_im)
-    fold_middle()
-
-    base = []
-    bases = []
-    for k in range(4):
+        put_part(w_own, k, core)
         rs_core[k].wait_recv()
 
         def add_core(b, carry, k=k):
@@ -591,180 +669,172 @@
             return carry
 
         lax.fori_loop(0, 16, add_core, 0, unroll=4)
-        base.append(0)
-        bases.append([])
-    offsets = [0, 8, 12, 14]
-
-    def rs_copy(k, s):
-        d = (k + s) % nd
-        size = 8 >> s
-        give = base[k] + (1 - bits[d]) * size
-        index = at["rs_xy"] + k * nd + s
-        return remote(
-            w_own.at[k, pl.ds(give, size)],
-            r_xy.at[k, pl.ds(offsets[s], size)],
-            index,
-            index,
-            cube[d],
-        )
-
-    for s in range(nd):
-        copies = [rs_copy(k, s) for k in range(4)]
-        for copy in copies:
+        for copy in rs_f(k):
             copy.start()
-        if s == 1:
-            fold_finish(light[...])
-        size = 8 >> s
-        for k in range(4):
-            copies[k].wait_recv()
-            bases[k].append(base[k])
-            keep = base[k] + bits[(k + s) % nd] * size
-            for b in range(size):
-                w_own[k, keep + b] = w_own[k, keep + b] + r_xy[k, offsets[s] + b]
-            base[k] = keep
-        for copy in copies:
-            copy.wait_send()
+    mass_next(1)
+    fold_middle()
     for k in range(4):
-        rs_core[k].wait_send()
+        for copy in rs_f(k):
+            copy.wait_recv()
+        mine = pl.ds(4 * f, 4)
+        w_own[k, mine] = w_own[k, mine] + (r_f[k, 0] + r_f[k, 1] + r_f[k, 2])
+        for copy in rs_g(k):
+            copy.start()
+    mass_next(2)
+    fold_finish(light[...])
     save = [
         pltpu.make_async_copy(tile.at[0], out_re, load_sem.at[0]),
         pltpu.make_async_copy(tile.at[1], out_im, load_sem.at[1]),
     ]
     for copy in save:
         copy.start()
-
-    left = 16 >> nd
-    per = 8 // nz
-
-    def part_of(slot):
-        return slot // 2, lax.rem(slot, 2)
-
-    def base_of(part):
-        value = base[0] * 0
-        for k in range(4):
-            value = value + (part == k).astype(jnp.int32) * base[k]
-        return value
-
-    def z_copy(k, q):
-        part, mode = part_of(z_at[k] * per + q)
-        index = at["rs_z"] + k * per + q
-        return remote(
-            w_own.at[part, pl.ds(base_of(part), left), pl.ds(2 * mode, 3)],
-            r_z.at[k, q],
-            index,
-            index,
-            z_dev[k],
-        )
-
-    def z_back(k, q):
-        part, mode = part_of(z * per + q)
-        where = af.at[core, part, pl.ds(base_of(part), left), mode]
-        index = at["ag_z"] + k * per + q
-        return remote(where, where, index, index, z_dev[k])
-
-    def z_back_recv(k, q):
-        part, mode = part_of(lax.rem(z + nz - k, nz) * per + q)
-        where = af.at[core, part, pl.ds(base_of(part), left), mode]
-        index = at["ag_z"] + k * per + q
-        return remote(where, where, index, index, z_dev[k])
-
+    for k in range(4):
+        for copy in rs_g(k):
+            copy.wait_recv()
+        w_own[k, spot] = w_own[k, spot] + (r_g[k, 0] + r_g[k, 1] + r_g[k, 2])
+        for mode in range(2):
+            pl.when(z != 2 * k + mode)(rs_z(k, mode).start)
+
+    part = z // 2
+    mode = lax.rem(z, 2)
+    r_z[z] = w_own[part, spot, pl.ds(2 * mode, 2)]
+    mass_next(3)
+    mass_here = wm[1, part, spot]
     for k in range(1, nz):
-        for q in range(per):
-            z_copy(k, q).start()
-    mass_sum = small_finish(1, len(groups) - 1, jnp.add)
-    mean_mass = jnp.sum(mass_sum) / (W * W)
-    for q in range(per):
-        part, mode = part_of(z * per + q)
-        first = base_of(part)
-        sums = []
-        for b in range(left):
-            sums.append([w_own[part, first + b, 2 * mode + e] for e in range(3)])
-        for k in range(1, nz):
-            z_copy(k, q).wait_recv()
-            for b in range(left):
-                for e in range(3):
-                    sums[b][e] = sums[b][e] + r_z[k, q, b, e]
-        for b in range(left):
-            spot = first + b
-            at_row = pl.multiple_of(part * Q + lax.rem(spot, 8) * 8, 8)
-            at_col = pl.multiple_of((spot // 8) * H, H)
-            first_is_re = jnp.broadcast_to(mode, (8, H)) == 0
-            mass_here = jnp.where(first_is_re, sums[b][2], sums[b][0])
-            g_re = jnp.where(first_is_re, sums[b][0], sums[b][1])
-            g_im = jnp.where(first_is_re, sums[b][1], sums[b][2])
-            scale = probe_step / (mass_here + mass_ratio * mean_mass)
-            m = 2 * core + mode
-            old_re = probe[m, pl.ds(at_row, 8), pl.ds(at_col, H)]
-            old_im = probe[MODES + m, pl.ds(at_row, 8), pl.ds(at_col, H)]
-            af[core, part, spot, mode, 0] = old_re + g_re * scale
-            af[core, part, spot, mode, 1] = old_im + g_im * scale
-        for k in range(1, nz):
-            z_back(k, q).start()
+        mass_here = mass_here + rm_z[k]
+    mean_mass = jnp.sum(small_finish(1, 3, jnp.add)) / (W * W)
+    scale = probe_step / (mass_here + mass_ratio * mean_mass)
+
+    def spot_rows(k, n):
+        start = k * Q
+        if n <= 32:
+            start = start + lax.rem(f, 2) * 32
+        if n <= 8:
+            start = start + g * 8
+        return pl.ds(pl.multiple_of(start, 8), n)
+
+    lanes = pl.ds(pl.multiple_of((f // 2) * H, H), H)
+    at_row = spot_rows(part, 8)
+    m = 2 * core + mode
+    old_re = probe[m, at_row, lanes]
+    old_im = probe[MODES + m, at_row, lanes]
+    for k in range(nz):
+        pl.when(z != k)(rs_z_from(k).wait_recv)
+    g_re = r_z[0, 0]
+    g_im = r_z[0, 1]
     for k in range(1, nz):
-        for q in range(per):
-            z_copy(k, q).wait_send()
-            z_back_recv(k, q).wait_recv()
-
-    def ag_copy(k, s):
-        d = (k + s) % nd
-        size = 8 >> s
-        mine = bases[k][s] + bits[d] * size
-        where = af.at[core, k, pl.ds(mine, size)]
-        index = at["ag_xy"] + k * nd + s
-        return remote(where, where, index, index, cube[d])
-
-    def ag_recv(k, s):
-        d = (k + s) % nd
-        size = 8 >> s
-        other = bases[k][s] + (1 - bits[d]) * size
-        where = af.at[core, k, pl.ds(other, size)]
-        index = at["ag_xy"] + k * nd + s
-        return remote(where, where, index, index, cube[d])
+        g_re = g_re + r_z[k, 0]
+        g_im = g_im + r_z[k, 1]
+    af[0, m, at_row, lanes] = old_re + g_re * scale
+    af[1, m, at_row, lanes] = old_im + g_im * scale
+
+    both = pl.ds(2 * core, 2)
+
+    def ag_z(to):
+        where = af.at[:, m, at_row, lanes]
+        return remote(where, where, at["ag_z"] + to, at["ag_z"] + z, dev_at(x, y, to, core))
+
+    def ag_z_from(k):
+        where = af.at[:, 2 * core + k % 2, spot_rows(k // 2, 8), lanes]
+        return remote(where, where, at["ag_z"] + k, at["ag_z"] + k, dev_at(x, y, k, core))
+
+    def ag_g(k):
+        where = af.at[:, both, spot_rows(k, 8), lanes]
+        first = at["ag_g"] + 3 * k - 1
+        return [remote(where, where, first + q, first + q, g_dev[q]) for q in range(1, 4)]
+
+    def ag_g_from(k):
+        first = at["ag_g"] + 3 * k - 1
+        copies = []
+        for q in range(1, 4):
+            start = k * Q + lax.rem(f, 2) * 32 + g_at[q] * 8
+            where = af.at[:, both, pl.ds(pl.multiple_of(start, 8), 8), lanes]
+            copies.append(remote(where, where, first + q, first + q, g_dev[q]))
+        return copies
+
+    def ag_f(k):
+        where = af.at[:, both, spot_rows(k, 32), lanes]
+        first = at["ag_f"] + 3 * k - 1
+        return [remote(where, where, first + q, first + q, f_dev[q]) for q in range(1, 4)]
+
+    def ag_f_from(k):
+        first = at["ag_f"] + 3 * k - 1
+        copies = []
+        for q in range(1, 4):
+            start = k * Q + lax.rem(f_at[q], 2) * 32
+            where = af.at[
+                :,
+                both,
+                pl.ds(pl.multiple_of(start, 32), 32),
+                pl.ds(pl.multiple_of((f_at[q] // 2) * H, H), H),
+            ]
+            copies.append(remote(where, where, first + q, first + q, f_dev[q]))
+        return copies
 
     def ag_core(k, which):
-        where = af.at[which, k]
+        where = af.at[:, pl.ds(2 * which, 2), k * Q : (k + 1) * Q]
         index = at["ag_core"] + k
         return remote(where, where, index, index, sibling)
 
-    for s in reversed(range(nd)):
-        for k in range(4):
-            ag_copy(k, s).start()
-        for k in range(4):
-            ag_recv(k, s).wait_recv()
-            if s == 0:
-                ag_core(k, core).start()
+    for k in range(nz):
+        pl.when(z != k)(ag_z(k).start)
+    for k in range(4):
+        for mode_k in range(2):
+            pl.when(z != 2 * k + mode_k)(ag_z_from(2 * k + mode_k).wait_recv)
+        for copy in ag_g(k):
+            copy.start()
+    for k in range(4):
+        for copy in ag_g_from(k):
+            copy.wait_recv()
+        for copy in ag_f(k):
+            copy.start()
+    for k in range(4):
+        for copy in ag_f_from(k):
+            copy.wait_recv()
+        ag_core(k, core).start()
     for k in range(4):
         ag_core(k, sib).wait_recv()
-    save.append(pltpu.make_async_copy(af, out_p, load_sem.at[2]))
-    save[-1].start()
-    for k in range(1, nz):
-        for q in range(per):
-            z_back(k, q).wait_send()
-    for s in range(nd):
-        for k in range(4):
-            ag_copy(k, s).wait_send()
+    save.append(pltpu.make_async_copy(af.at[0], out_pre, load_sem.at[2]))
+    save.append(pltpu.make_async_copy(af.at[1], out_pim, load_sem.at[3]))
+    save[2].start()
+    save[3].start()
+
     for k in range(4):
+        rs_core[k].wait_send()
         ag_core(k, core).wait_send()
+        for copy in rs_f(k) + rs_g(k) + ag_g(k) + ag_f(k):
+            copy.wait_send()
+    for k in range(nz):
+        pl.when(z != k)(rs_z(k // 2, k % 2).wait_send)
+        pl.when(z != k)(ag_z(k).wait_send)
     for copy in save:
         copy.wait()
 
 
+def write_out(*refs):
+    sem = refs[-1]
+    copies = [pltpu.make_async_copy(refs[i], refs[4 + i], sem.at[i]) for i in range(4)]
+    for copy in copies:
+        copy.start()
+    for copy in copies:
+        copy.wait()
+
+
 def local(n_row, n_col, obj_re, obj_im, probe_re, probe_im, amps, positions):
-    ny, nz, nd, n_small, at, n_sems = layout(n_row, n_col)
+    n_small, at, n_sems = layout()
     right, left = make_pairs()
-    any_spec = pl.BlockSpec(memory_space=pl.ANY)
-    n_groups = 4 if ny == 4 else 3
-    keep = 16 >> nd
-    per = 8 // nz
-    out_re, out_im, out_p = pl.pallas_call(
+    any_spec = pl.BlockSpec(memory_space=pltpu.HBM)
+    shapes = (
+        jax.ShapeDtypeStruct((H, H), f32),
+        jax.ShapeDtypeStruct((H, H), f32),
+        jax.ShapeDtypeStruct((MODES, W, W), f32),
+        jax.ShapeDtypeStruct((MODES, W, W), f32),
+    )
+    results = pl.pallas_call(
         functools.partial(kernel, n_row, n_col),
-        out_shape=(
-            jax.ShapeDtypeStruct((H, H), f32),
-            jax.ShapeDtypeStruct((H, H), f32),
-            jax.ShapeDtypeStruct((2, 4, 16, 2, 2, 8, H), f32),
-        ),
+        out_shape=shapes,
         in_specs=[pl.BlockSpec(memory_space=pltpu.SMEM)] + [any_spec] * 7,
-        out_specs=(any_spec, any_spec, any_spec),
+        out_specs=(any_spec,) * 4,
         scratch_shapes=[
             pltpu.VMEM((2, H, H), f32),
             pltpu.VMEM((2 * MODES, W, W), f32),
@@ -788,20 +858,26 @@
             pltpu.VMEM((3, 3, 8, H), jnp.int32),
             pltpu.VMEM((2 * W, 2 * W), f32),
             pltpu.VMEM((2 * W, 2 * W), f32),
-            pltpu.VMEM((2, n_groups, 8, H), f32),
+            pltpu.VMEM((2, 4, 8, H), f32),
             pltpu.VMEM((2, n_small, 8, H), f32),
-            pltpu.VMEM((4, 16, 5, 8, H), f32),
-            pltpu.VMEM((4, 16, 5, 8, H), f32),
-            pltpu.VMEM((4, 16, 5, 8, H), f32),
-            pltpu.VMEM((4, 15, 5, 8, H), f32),
-            pltpu.VMEM((nz, per, keep, 3, 8, H), f32),
-            pltpu.VMEM((2, 4, 16, 2, 2, 8, H), f32),
+            pltpu.VMEM((4, 16, 4, 8, H), f32),
+            pltpu.VMEM((4, 16, 4, 8, H), f32),
+            pltpu.VMEM((4, 16, 4, 8, H), f32),
+            pltpu.VMEM((4, 3, 4, 4, 8, H), f32),
+            pltpu.VMEM((4, 3, 4, 8, H), f32),
+            pltpu.VMEM((NZ, 2, 8, H), f32),
+            pltpu.VMEM((2, 4, 16, 8, H), f32),
+            pltpu.VMEM((4, 16, 8, H), f32),
+            pltpu.VMEM((3, 4, 4, 8, H), f32),
+            pltpu.VMEM((3, 4, 1, 8, H), f32),
+            pltpu.VMEM((NZ, 8, H), f32),
+            pltpu.VMEM((2, MODES, W, W), f32),
             pltpu.SemaphoreType.DMA((7,)),
             pltpu.SemaphoreType.DMA((n_sems,)),
             pltpu.SemaphoreType.DMA((n_sems,)),
         ],
         compiler_params=pltpu.CompilerParams(
-            collective_id=0, has_side_effects=True, vmem_limit_bytes=48 << 20
+            collective_id=0, has_side_effects=True, vmem_limit_bytes=60 << 20
         ),
     )(
         positions.reshape(1, 2),
@@ -813,9 +889,13 @@
         jnp.asarray(right),
         jnp.asarray(left),
     )
-    parts = out_p.reshape(2, 4, 2, 8, 2, 2, 8, H)
-    new = parts.transpose(5, 0, 4, 1, 3, 6, 2, 7).reshape(2, MODES, W, W)
-    return (out_re, out_im, new[0], new[1])
+    return pl.pallas_call(
+        write_out,
+        out_shape=shapes,
+        in_specs=[any_spec] * 4,
+        out_specs=(any_spec,) * 4,
+        scratch_shapes=[pltpu.SemaphoreType.DMA((4,))],
+    )(*results)
 
 
 def solution(mesh):

time: 153 us -> 190 us (1.24)
  Pallas kernels: 141 us -> 189 us
  local copies, waits for them, and re-layouts: 11.5 us -> 0 us
    pallas_call x1 -> x2, Pallas kernels: 141 us -> 189 us  [the longest x1 120 us: local(): pl.pallas_call(functools.partial(kernel, n_row, n_col), out_shape=shapes,...]
    unnamed x18 -> x0, local copies, waits for them, and re-layouts: 9.06 us -> none
    slice x3 -> x0, local copies, waits for them, and re-layouts: 2.4 us -> none  [local(): return (out_re, out_im, new[0], new[1])]
where the time goes in v2:
time: 190 us
  Pallas kernels  189 us (99%)
    pallas_call x1, Pallas kernels, local(): pl.pallas_call(functools.partial(kernel, n_row, n_col), out_shape=shapes,...  120 us
    pallas_call x1, Pallas kernels, local(): pl.pallas_call(write_out, out_shape=shapes, in_specs=[any_spec] * 4, out_...  68.6 us

profile of v2, /device:TPU:1, one launch (start us, length us, event | category | flops | bytes accessed | tf_op | source)
XLA Modules:
  0.0 189.6 jit_solution(13716947753717723057)
XLA Ops:
  0.6 120.3 %shard_map.111 = (f32[128,128]{1,0:T(8,128)}, f32[128,128]{1,0:T(8,128)}, f32[4,256,256]{2,1,0:T(8,128)}, f32[4,256,256]{2,1,0:T(8,128)}) custom-call(s32[1,2]{1,0:T(1,128)} %bitcast.3, f32[128,128]{1,0:T(8,128)} %ore_ref.1, f32[128,128]{1,0:T(8,128)} %oim_ref.1, f32[4,256,256]{2,1,0:T(8,128)} %pre_ref.1, f32[4,256,256]{2,1,0:T(8,128)} %pim_ref.1, ...), custom_call_target="tpu_custom_call" | custom-call | tf_op jit(solution)/shard_map/pallas_call | solution.py:833
  120.9 68.6 %shard_map.112 = (f32[128,128]{1,0:T(8,128)}, f32[128,128]{1,0:T(8,128)}, f32[4,256,256]{2,1,0:T(8,128)}, f32[4,256,256]{2,1,0:T(8,128)}) custom-call(f32[128,128]{1,0:T(8,128)} %get-tuple-element.8.refs_0_, f32[128,128]{1,0:T(8,128)} %get-tuple-element.9.refs_1_, f32[4,256,256]{2,1,0:T(8,128)} %get-tuple-element.10.refs_2_, ...), custom_call_target="tpu_custom_call" | custom-call | tf_op jit(solution)/shard_map/pallas_call | solution.py:892

commit v3 on v2

--- a/solution.py
+++ b/solution.py
@@ -47,13 +47,16 @@
 
 
 NX, NY, NZ = 4, 4, 8
+CHUNKS = 2
 
 
 def layout():
     sems = Sems()
     at = {}
-    for name in ("pos_r", "pos_c", "halo_r", "halo_o", "halo_s", "fold_a", "fold_b", "fold_r"):
+    for name in ("pos_r", "pos_c", "halo_o", "fold_b"):
         at[name] = sems.take(2)
+    for name in ("halo_r", "halo_s", "fold_a", "fold_r"):
+        at[name] = sems.take(2 * CHUNKS)
     small = 1 + 3 + 3 + 7
     at["small"] = [sems.take(small), sems.take(small)]
     at["mass"] = sems.take(small + 1)
@@ -244,12 +247,28 @@
 
     pos_r = Pair("v", [posb.at[1, 1]] * 2, lambda d: posb.at[1, 2 * d], at["pos_r"])
     pos_c = Pair("h", [posb.at[1]] * 2, lambda d: posb.at[2 * d], at["pos_c"])
-    halo_r = Pair("v", [tile] * 2, lambda d: hv.at[d], at["halo_r"])
+    rows_of = [slice(n * (H // CHUNKS), (n + 1) * (H // CHUNKS)) for n in range(CHUNKS)]
+
+    def chunked(axis, src_of, dst_of, first):
+        pairs = []
+        for n in range(CHUNKS):
+            rows = pl.ds(n * (H // CHUNKS), H // CHUNKS)
+            pairs.append(
+                Pair(
+                    axis,
+                    [src_of(d).at[:, rows] for d in range(2)],
+                    lambda d, rows=rows: dst_of(d).at[:, rows],
+                    first + 2 * n,
+                )
+            )
+        return pairs
+
     halo_o = Pair("h", [tile] * 2, lambda d: hh.at[d, 1], at["halo_o"])
-    halo_s = Pair("h", [sh.at[0], sh.at[1]], lambda d: hh.at[d, 0], at["halo_s"])
-    fold_a = Pair("h", [fs.at[0, 0], fs.at[1, 0]], lambda d: fr.at[d, 0], at["fold_a"])
+    halo_r = chunked("v", lambda d: tile, lambda d: hv.at[d], at["halo_r"])
+    halo_s = chunked("h", lambda d: sh.at[d], lambda d: hh.at[d, 0], at["halo_s"])
     fold_b = Pair("h", [fs.at[0, 1], fs.at[1, 1]], lambda d: fr.at[d, 1], at["fold_b"])
-    fold_r = Pair("v", [us.at[0], us.at[1]], lambda d: ur.at[d], at["fold_r"])
+    fold_a = chunked("h", lambda d: fs.at[d, 0], lambda d: fr.at[d, 0], at["fold_a"])
+    fold_r = chunked("v", lambda d: us.at[d], lambda d: ur.at[d], at["fold_r"])
 
     def near_lr(d):
         return (posb[2 * d, 1][0:1, :] // 4) * Q
@@ -287,19 +306,21 @@
         small_start(which, g + 1, small_finish(which, g, op))
 
     def halo_start():
-        halo_r.start()
+        for pair in halo_r:
+            pair.start()
         halo_o.start()
 
     def nothing():
         pass
 
-    def halo_finish(first=nothing, second=nothing):
-        halo_r.recv()
-        for d in range(2):
-            pick = rows_i < near_lr(d)
-            for c in range(2):
-                sh[d, c] = jnp.where(pick, hv[1, c], hv[0, c])
-            halo_s.start(d)
+    def halo_to_half(first=nothing, second=nothing):
+        for n, rows in enumerate(rows_of):
+            halo_r[n].recv()
+            for d in range(2):
+                pick = rows_i[rows] < near_lr(d)
+                for c in range(2):
+                    sh[d, c, rows] = jnp.where(pick, hv[1, c, rows], hv[0, c, rows])
+                halo_s[n].start(d)
         first()
         for c in range(2):
             win[c, H:, H:] = tile[c]
@@ -307,13 +328,37 @@
         halo_o.recv()
         for c in range(2):
             win[c, H:, :H] = jnp.where(right_of, hh[1, 1, c], hh[0, 1, c])
+        half_block(2)
+        half_block(3)
         second()
-        halo_s.recv()
-        for c in range(2):
-            win[c, :H, :H] = jnp.where(right_of, hh[1, 0, c], hh[0, 0, c])
-        halo_r.sent()
-        halo_o.sent()
-        halo_s.sent()
+        for n, rows in enumerate(rows_of):
+            halo_s[n].recv()
+            for c in range(2):
+                win[c, rows, :H] = jnp.where(right_of[rows], hh[1, 0, c, rows], hh[0, 0, c, rows])
+            half_block(n)
+        for pair in halo_r + [halo_o] + halo_s:
+            pair.sent()
+
+    def half_block(b):
+        for r in range(0, Q, step_rows):
+            here = slice(b * Q + r, b * Q + r + step_rows)
+            wr, wi = win[0, here, :], win[1, here, :]
+            for m in range(MODES):
+                pr, pi = prot[m, here, :], prot[MODES + m, here, :]
+                there = slice(b * W + m * Q + r, b * W + m * Q + r + step_rows)
+                psi[there, 0:W] = (pr * wr - pi * wi).astype(bf16)
+                psi[there, W:] = (pr * wi + pi * wr).astype(bf16)
+        for part in range(2):
+            out = jnp.dot(
+                psi[b * W : (b + 1) * W, :],
+                m1[:, part * W : (part + 1) * W],
+                preferred_element_type=f32,
+            ).astype(bf16)
+            for m in range(MODES):
+                at_row = part * W + b * Q
+                hs[m, at_row : at_row + Q] = out[m * Q : (m + 1) * Q]
+
+    step_rows = 32
 
     def product_right(table):
         for part in range(2):
@@ -326,22 +371,6 @@
     def product_left(table):
         for m in range(MODES):
             spec[m] = jnp.dot(table[...], hs[m], preferred_element_type=f32)
-
-    step_rows = 32
-
-    def make_psi():
-        def body(i, carry):
-            at_row = pl.multiple_of(i * step_rows, step_rows)
-            here = pl.ds(at_row, step_rows)
-            wr, wi = win[0, here, :], win[1, here, :]
-            for m in range(MODES):
-                pr, pi = prot[m, here, :], prot[MODES + m, here, :]
-                there = pl.ds(pl.multiple_of(m * W + at_row, step_rows), step_rows)
-                psi[there, 0:W] = (pr * wr - pi * wi).astype(bf16)
-                psi[there, W:] = (pr * wi + pi * wr).astype(bf16)
-            return carry
-
-        lax.fori_loop(0, W // step_rows, body, 0)
 
     def make_change():
         def body(i, carry):
@@ -361,11 +390,10 @@
 
         lax.fori_loop(0, W // step_rows, body, 0)
 
-    def make_grad():
-        def body(i, carry):
-            at_row = pl.multiple_of(i * step_rows, step_rows)
-            here = pl.ds(at_row, step_rows)
-            here_im = pl.ds(pl.multiple_of(W + at_row, step_rows), step_rows)
+    def make_grad(rows):
+        for r in range(rows.start, rows.stop, step_rows):
+            here = slice(r, r + step_rows)
+            here_im = slice(W + r, W + r + step_rows)
             g_re = jnp.zeros((step_rows, W), f32)
             g_im = jnp.zeros((step_rows, W), f32)
             for m in range(MODES):
@@ -375,44 +403,53 @@
                 g_im = g_im + (pr * ei - pi * er)
             grad[0, here, :] = g_re
             grad[1, here, :] = g_im
-            return carry
-
-        lax.fori_loop(0, W // step_rows, body, 0)
 
     def fold_start():
         zero = jnp.zeros((H, H), f32)
-        for part in range(2):
-            half = slice(0, H) if part == 0 else slice(H, W)
+        for n, rows in enumerate(rows_of):
+            make_grad(rows)
             for c in range(2):
-                g = grad[c, half, :H]
-                fs[0, part, c] = jnp.where(right_of, zero, g)
-                fs[1, part, c] = jnp.where(right_of, g, zero)
-            (fold_a, fold_b)[part].start()
+                fs[0, 0, c, rows] = jnp.where(right_of[rows], zero[rows], grad[c, rows, :H])
+                fs[1, 0, c, rows] = jnp.where(right_of[rows], grad[c, rows, :H], zero[rows])
+            fold_a[n].start()
+        make_grad(slice(H, W))
+        for c in range(2):
+            fs[0, 1, c] = jnp.where(right_of, zero, grad[c, H:, :H])
+            fs[1, 1, c] = jnp.where(right_of, grad[c, H:, :H], zero)
+        fold_b.start()
 
     def fold_middle(first=nothing):
         first()
-        fold_a.recv()
-        zero = jnp.zeros((H, H), f32)
-        picks = [below, rows_i < near_lr(0), rows_i < near_lr(1)]
-        for c in range(2):
-            parts = [grad[c, :H, H:], fr[0, 0, c], fr[1, 0, c]]
-            up, down = zero, zero
-            for pick, part in zip(picks, parts):
-                up = up + jnp.where(pick, zero, part)
-                down = down + jnp.where(pick, part, zero)
-            us[0, c] = up
-            us[1, c] = down
-        fold_r.start()
-
-    def fold_finish(denom):
+        for n, rows in enumerate(rows_of):
+            fold_a[n].recv()
+            here = rows_i[rows]
+            picks = [here < lr, here < near_lr(0), here < near_lr(1)]
+            for c in range(2):
+                parts = [grad[c, rows, H:], fr[0, 0, c, rows], fr[1, 0, c, rows]]
+                up = jnp.zeros((H // CHUNKS, H), f32)
+                down = up
+                for pick, part in zip(picks, parts):
+                    up = up + jnp.where(pick, 0.0, part)
+                    down = down + jnp.where(pick, part, 0.0)
+                us[0, c, rows] = up
+                us[1, c, rows] = down
+            fold_r[n].start()
+
+    def fold_finish(denom, again):
         fold_b.recv()
-        fold_r.recv()
-        for c in range(2):
-            total = grad[c, H:, H:] + fr[0, 1, c] + fr[1, 1, c] + ur[0, c] + ur[1, c]
-            tile[c] = tile[c] + total / denom
-        fold_a.sent()
-        fold_b.sent()
-        fold_r.sent()
+        for n, rows in enumerate(rows_of):
+            own = slice(H + rows.start, H + rows.stop)
+            sides = [grad[c, own, H:] + fr[0, 1, c, rows] + fr[1, 1, c, rows] for c in range(2)]
+            fold_r[n].recv()
+            for c in range(2):
+                total = sides[c] + ur[0, c, rows] + ur[1, c, rows]
+                tile[c, rows] = tile[c, rows] + total / denom[rows]
+            if again:
+                halo_r[n].start()
+        if again:
+            halo_o.start()
+        for pair in fold_a + [fold_b] + fold_r:
+            pair.sent()
 
     loads[0].wait()
     loads[1].wait()
@@ -492,34 +529,28 @@
                 peak = jnp.maximum(peak, total[k * 8 : (k + 1) * 8, :])
         small_start(0, 0, peak)
 
-    def one_pass(first=nothing, second=nothing):
-        make_psi()
-        product_right(m1)
-        first()
+    def transforms(first=nothing):
         product_left(m2)
         make_change()
         product_right(m2)
-        second()
+        first()
         product_left(m1)
-        make_grad()
-
-    halo_finish(make_light, lambda: small_next(0, 0, jnp.maximum))
-    one_pass(nothing, lambda: small_next(0, 1, jnp.maximum))
+
+    halo_to_half(make_light, lambda: small_next(0, 0, jnp.maximum))
+    transforms(lambda: small_next(0, 1, jnp.maximum))
     fold_start()
     fold_middle(lambda: small_next(0, 2, jnp.maximum))
     peak = small_finish(0, 3, jnp.maximum)
     light[...] = light[...] + light_ratio * jnp.max(peak)
-    fold_finish(light[...])
-
-    halo_start()
-    halo_finish()
-    one_pass()
+    fold_finish(light[...], True)
+
+    halo_to_half()
+    transforms()
     fold_start()
     fold_middle()
-    fold_finish(light[...])
-
-    halo_start()
-    halo_finish()
+    fold_finish(light[...], True)
+
+    halo_to_half()
     spot = 4 * f + g
 
     def mass_copies(stage):
@@ -588,22 +619,24 @@
         put(store_mass, turned([grad[0, block(k + t), :] for t in range(3)], True))
     mass_copies(0)[0].start()
 
-    one_pass(nothing, lambda: mass_next(0))
+    transforms(lambda: mass_next(0))
     fold_start()
 
     sib = 1 - core
 
-    def mode_products(m, carry):
-        for b in range(4):
-            here = block(b)
-            here_im = slice(W + b * Q, W + b * Q + Q)
-            wr, wi = win[0, here, :], win[1, here, :]
-            er, ei = spec[m, here, :], spec[m, here_im, :]
-            spec[m, here, :] = wr * er + wi * ei
-            spec[m, here_im, :] = wr * ei - wi * er
-        return carry
-
-    lax.fori_loop(0, MODES, mode_products, 0)
+    def mode_products(which):
+        def body(mm, carry):
+            m = 2 * which + mm
+            for b in range(4):
+                here = block(b)
+                here_im = slice(W + b * Q, W + b * Q + Q)
+                wr, wi = win[0, here, :], win[1, here, :]
+                er, ei = spec[m, here, :], spec[m, here_im, :]
+                spec[m, here, :] = wr * er + wi * ei
+                spec[m, here_im, :] = wr * ei - wi * er
+            return carry
+
+        lax.fori_loop(0, 2, body, 0)
 
     def put_part(target, k, which):
         for mm in range(2):
@@ -627,9 +660,11 @@
         remote(w_sib.at[k], r_core.at[k], at["rs_core"] + k, at["rs_core"] + k, sibling)
         for k in range(4)
     ]
+    mode_products(sib)
     for k in range(4):
         put_part(w_sib, k, sib)
         rs_core[k].start()
+    mode_products(core)
 
     def rs_f(k):
         first = at["rs_f"] + 3 * k - 1
@@ -681,7 +716,7 @@
         for copy in rs_g(k):
             copy.start()
     mass_next(2)
-    fold_finish(light[...])
+    fold_finish(light[...], False)
     save = [
         pltpu.make_async_copy(tile.at[0], out_re, load_sem.at[0]),
         pltpu.make_async_copy(tile.at[1], out_im, load_sem.at[1]),
@@ -811,12 +846,19 @@
         copy.wait()
 
 
-def write_out(*refs):
-    sem = refs[-1]
-    copies = [pltpu.make_async_copy(refs[i], refs[4 + i], sem.at[i]) for i in range(4)]
-    for copy in copies:
+def write_out(ore, oim, opre, opim, nre, nim, npre, npim, small, large, sem):
+    steps = [(ore, nre, small.at[0]), (oim, nim, small.at[1])]
+    for c, (src, dst) in enumerate(((opre, npre), (opim, npim))):
+        for m in range(MODES):
+            steps.append((src.at[m], dst.at[m], large.at[c, m]))
+    reads = [pltpu.make_async_copy(a, b, sem.at[0, n]) for n, (a, _, b) in enumerate(steps)]
+    writes = [pltpu.make_async_copy(b, a, sem.at[1, n]) for n, (_, a, b) in enumerate(steps)]
+    for copy in reads:
         copy.start()
-    for copy in copies:
+    for read, write in zip(reads, writes):
+        read.wait()
+        write.start()
+    for copy in writes:
         copy.wait()
 
 
@@ -894,7 +936,11 @@
         out_shape=shapes,
         in_specs=[any_spec] * 4,
         out_specs=(any_spec,) * 4,
-        scratch_shapes=[pltpu.SemaphoreType.DMA((4,))],
+        scratch_shapes=[
+            pltpu.VMEM((2, H, H), f32),
+            pltpu.VMEM((2, MODES, W, W), f32),
+            pltpu.SemaphoreType.DMA((2, 2 + 2 * MODES)),
+        ],
     )(*results)
 
 

time: 190 us -> 119 us (0.63)
  Pallas kernels: 189 us -> 118 us
    pallas_call x1, Pallas kernels: 68.6 us -> 2.51 us  [local(): pl.pallas_call(write_out, out_shape=shapes, in_specs=[any_spec] * 4, out_...]
    pallas_call x1, Pallas kernels: 120 us -> 116 us  [local(): pl.pallas_call(functools.partial(kernel, n_row, n_col), out_shape=shapes,...]
where the time goes in v3:
time: 119 us
  Pallas kernels  118 us (99%)
    pallas_call x1, Pallas kernels, local(): pl.pallas_call(functools.partial(kernel, n_row, n_col), out_shape=shapes,...  116 us
    pallas_call x1, Pallas kernels, local(): pl.pallas_call(write_out, out_shape=shapes, in_specs=[any_spec] * 4, out_...  2.51 us

profile of v3, /device:TPU:1, one launch (start us, length us, event | category | flops | bytes accessed | tf_op | source)
XLA Modules:
  0.0 118.8 jit_solution(7785078602523248272)
XLA Ops:
  0.6 115.6 %shard_map.111 = (f32[128,128]{1,0:T(8,128)}, f32[128,128]{1,0:T(8,128)}, f32[4,256,256]{2,1,0:T(8,128)}, f32[4,256,256]{2,1,0:T(8,128)}) custom-call(s32[1,2]{1,0:T(1,128)} %bitcast.3, f32[128,128]{1,0:T(8,128)} %ore_ref.1, f32[128,128]{1,0:T(8,128)} %oim_ref.1, f32[4,256,256]{2,1,0:T(8,128)} %pre_ref.1, f32[4,256,256]{2,1,0:T(8,128)} %pim_ref.1, ...), custom_call_target="tpu_custom_call" | custom-call | tf_op jit(solution)/shard_map/pallas_call | solution.py:875
  116.3 2.5 %shard_map.112 = (f32[128,128]{1,0:T(8,128)}, f32[128,128]{1,0:T(8,128)}, f32[4,256,256]{2,1,0:T(8,128)}, f32[4,256,256]{2,1,0:T(8,128)}) custom-call(f32[128,128]{1,0:T(8,128)} %get-tuple-element.8.ore, f32[128,128]{1,0:T(8,128)} %get-tuple-element.9.oim, f32[4,256,256]{2,1,0:T(8,128)} %get-tuple-element.10.opre, f32[4,256,256]{2,1,0:T(8,128)} %get-tuple-element.11.opim), custom_call_target="tpu_custom_call" | custom-call | tf_op jit(solution)/shard_map/pallas_call | solution.py:934

commit v4 on v3

--- a/solution.py
+++ b/solution.py
@@ -53,7 +53,7 @@
 def layout():
     sems = Sems()
     at = {}
-    for name in ("pos_r", "pos_c", "halo_o", "fold_b"):
+    for name in ("pos_h", "pos_r", "pos_c", "halo_o", "fold_b"):
         at[name] = sems.take(2)
     for name in ("halo_r", "halo_s", "fold_a", "fold_r"):
         at[name] = sems.take(2 * CHUNKS)
@@ -82,11 +82,8 @@
     amp_ref,
     m1_ref,
     m2_ref,
-    out_re,
-    out_im,
-    out_pre,
-    out_pim,
     tile,
+    af,
     probe,
     prot,
     amps,
@@ -97,6 +94,7 @@
     psi,
     hs,
     spec,
+    prod,
     hv,
     hh,
     sh,
@@ -106,6 +104,7 @@
     ur,
     light,
     posb,
+    posh,
     padded,
     padded64,
     sm_send,
@@ -121,7 +120,6 @@
     rm_f,
     rm_g,
     rm_z,
-    af,
     load_sem,
     send_sem,
     recv_sem,
@@ -223,6 +221,7 @@
     for dj in range(3):
         for di in range(3):
             posb[dj, di] = jnp.full((8, 128), 4 * di + dj, jnp.int32)
+    posh[...] = jnp.zeros_like(posh)
     posb[1, 1] = jnp.broadcast_to(4 * a_r + a_c, (8, 128)).astype(jnp.int32)
 
     barrier = pltpu.get_barrier_semaphore()
@@ -245,6 +244,7 @@
     below = rows_i < lr
     right_of = cols_i < lc
 
+    pos_h = Pair("h", [posb.at[1, 1]] * 2, lambda d: posh.at[d], at["pos_h"])
     pos_r = Pair("v", [posb.at[1, 1]] * 2, lambda d: posb.at[1, 2 * d], at["pos_r"])
     pos_c = Pair("h", [posb.at[1]] * 2, lambda d: posb.at[2 * d], at["pos_c"])
     rows_of = [slice(n * (H // CHUNKS), (n + 1) * (H // CHUNKS)) for n in range(CHUNKS)]
@@ -271,7 +271,7 @@
     fold_r = chunked("v", lambda d: us.at[d], lambda d: ur.at[d], at["fold_r"])
 
     def near_lr(d):
-        return (posb[2 * d, 1][0:1, :] // 4) * Q
+        return (posh[d][0:1, :] // 4) * Q
 
     groups = [[sibling], f_dev[1:], g_dev[1:], z_dev[1:]]
     small_first = [0]
@@ -368,8 +368,8 @@
             for m in range(MODES):
                 hs[m, part * W : (part + 1) * W] = out[m * W : (m + 1) * W]
 
-    def product_left(table):
-        for m in range(MODES):
+    def product_left(table, modes=range(MODES)):
+        for m in modes:
             spec[m] = jnp.dot(table[...], hs[m], preferred_element_type=f32)
 
     def make_change():
@@ -451,9 +451,10 @@
         for pair in fold_a + [fold_b] + fold_r:
             pair.sent()
 
+    pos_h.start()
+    pos_r.start()
     loads[0].wait()
     loads[1].wait()
-    pos_r.start()
     halo_start()
     loads[2].wait()
     loads[3].wait()
@@ -491,13 +492,18 @@
         rows = slice(b * Q, (b + 1) * Q)
         padded64[rows, :] = pltpu.roll(padded[rows, :], Q, 1)
 
+    for load in loads[4:]:
+        load.wait()
+    pos_h.recv()
     pos_r.recv()
     pos_c.start()
-    for load in loads[4:]:
-        load.wait()
-    pos_c.recv()
-    pos_r.sent()
-    pos_c.sent()
+
+    def settle_light():
+        pos_c.recv()
+        pos_h.sent()
+        pos_r.sent()
+        pos_c.sent()
+        make_light()
 
     def make_light():
         peak = jnp.full((8, H), 0.0, f32)
@@ -536,7 +542,7 @@
         first()
         product_left(m1)
 
-    halo_to_half(make_light, lambda: small_next(0, 0, jnp.maximum))
+    halo_to_half(settle_light, lambda: small_next(0, 0, jnp.maximum))
     transforms(lambda: small_next(0, 1, jnp.maximum))
     fold_start()
     fold_middle(lambda: small_next(0, 2, jnp.maximum))
@@ -619,8 +625,10 @@
         put(store_mass, turned([grad[0, block(k + t), :] for t in range(3)], True))
     mass_copies(0)[0].start()
 
-    transforms(lambda: mass_next(0))
-    fold_start()
+    product_left(m2)
+    make_change()
+    product_right(m2)
+    mass_next(0)
 
     sib = 1 - core
 
@@ -632,8 +640,8 @@
                 here_im = slice(W + b * Q, W + b * Q + Q)
                 wr, wi = win[0, here, :], win[1, here, :]
                 er, ei = spec[m, here, :], spec[m, here_im, :]
-                spec[m, here, :] = wr * er + wi * ei
-                spec[m, here_im, :] = wr * ei - wi * er
+                prod[m, here, :] = wr * er + wi * ei
+                prod[m, here_im, :] = wr * ei - wi * er
             return carry
 
         lax.fori_loop(0, 2, body, 0)
@@ -649,7 +657,7 @@
                     store,
                     turned(
                         [
-                            spec[2 * which + mm, pl.ds(c * W + ((k + t) % 4) * Q, Q), :]
+                            prod[2 * which + mm, pl.ds(c * W + ((k + t) % 4) * Q, Q), :]
                             for t in range(3)
                         ],
                         True,
@@ -660,10 +668,12 @@
         remote(w_sib.at[k], r_core.at[k], at["rs_core"] + k, at["rs_core"] + k, sibling)
         for k in range(4)
     ]
+    product_left(m1, [2 * sib, 2 * sib + 1])
     mode_products(sib)
     for k in range(4):
         put_part(w_sib, k, sib)
         rs_core[k].start()
+    product_left(m1, [2 * core, 2 * core + 1])
     mode_products(core)
 
     def rs_f(k):
@@ -706,6 +716,7 @@
         lax.fori_loop(0, 16, add_core, 0, unroll=4)
         for copy in rs_f(k):
             copy.start()
+    fold_start()
     mass_next(1)
     fold_middle()
     for k in range(4):
@@ -717,12 +728,6 @@
             copy.start()
     mass_next(2)
     fold_finish(light[...], False)
-    save = [
-        pltpu.make_async_copy(tile.at[0], out_re, load_sem.at[0]),
-        pltpu.make_async_copy(tile.at[1], out_im, load_sem.at[1]),
-    ]
-    for copy in save:
-        copy.start()
     for k in range(4):
         for copy in rs_g(k):
             copy.wait_recv()
@@ -829,11 +834,6 @@
         ag_core(k, core).start()
     for k in range(4):
         ag_core(k, sib).wait_recv()
-    save.append(pltpu.make_async_copy(af.at[0], out_pre, load_sem.at[2]))
-    save.append(pltpu.make_async_copy(af.at[1], out_pim, load_sem.at[3]))
-    save[2].start()
-    save[3].start()
-
     for k in range(4):
         rs_core[k].wait_send()
         ag_core(k, core).wait_send()
@@ -842,23 +842,14 @@
     for k in range(nz):
         pl.when(z != k)(rs_z(k // 2, k % 2).wait_send)
         pl.when(z != k)(ag_z(k).wait_send)
-    for copy in save:
-        copy.wait()
-
-
-def write_out(ore, oim, opre, opim, nre, nim, npre, npim, small, large, sem):
-    steps = [(ore, nre, small.at[0]), (oim, nim, small.at[1])]
-    for c, (src, dst) in enumerate(((opre, npre), (opim, npim))):
-        for m in range(MODES):
-            steps.append((src.at[m], dst.at[m], large.at[c, m]))
-    reads = [pltpu.make_async_copy(a, b, sem.at[0, n]) for n, (a, _, b) in enumerate(steps)]
-    writes = [pltpu.make_async_copy(b, a, sem.at[1, n]) for n, (_, a, b) in enumerate(steps)]
-    for copy in reads:
+
+
+def write_out(tile, af, new_re, new_im, new_pre, new_pim, sem):
+    pairs = [(af.at[0], new_pre), (af.at[1], new_pim), (tile.at[0], new_re), (tile.at[1], new_im)]
+    copies = [pltpu.make_async_copy(a, b, sem.at[n]) for n, (a, b) in enumerate(pairs)]
+    for copy in copies:
         copy.start()
-    for read, write in zip(reads, writes):
-        read.wait()
-        write.start()
-    for copy in writes:
+    for copy in copies:
         copy.wait()
 
 
@@ -874,11 +865,10 @@
     )
     results = pl.pallas_call(
         functools.partial(kernel, n_row, n_col),
-        out_shape=shapes,
+        out_shape=(pltpu.VMEM((2, H, H), f32), pltpu.VMEM((2, MODES, W, W), f32)),
         in_specs=[pl.BlockSpec(memory_space=pltpu.SMEM)] + [any_spec] * 7,
-        out_specs=(any_spec,) * 4,
+        out_specs=(pl.BlockSpec(memory_space=pltpu.VMEM),) * 2,
         scratch_shapes=[
-            pltpu.VMEM((2, H, H), f32),
             pltpu.VMEM((2 * MODES, W, W), f32),
             pltpu.VMEM((2 * MODES, W, W), f32),
             pltpu.VMEM((W, W), f32),
@@ -889,6 +879,7 @@
             pltpu.VMEM((MODES * W, 2 * W), bf16),
             pltpu.VMEM((MODES, 2 * W, W), bf16),
             pltpu.VMEM((MODES, 2 * W, W), f32),
+            pltpu.VMEM((MODES, 2 * W, W), f32),
             pltpu.VMEM((2, 2, H, H), f32),
             pltpu.VMEM((2, 2, 2, H, H), f32),
             pltpu.VMEM((2, 2, H, H), f32),
@@ -898,6 +889,7 @@
             pltpu.VMEM((2, 2, H, H), f32),
             pltpu.VMEM((H, H), f32),
             pltpu.VMEM((3, 3, 8, H), jnp.int32),
+            pltpu.VMEM((2, 8, H), jnp.int32),
             pltpu.VMEM((2 * W, 2 * W), f32),
             pltpu.VMEM((2 * W, 2 * W), f32),
             pltpu.VMEM((2, 4, 8, H), f32),
@@ -913,7 +905,6 @@
             pltpu.VMEM((3, 4, 4, 8, H), f32),
             pltpu.VMEM((3, 4, 1, 8, H), f32),
             pltpu.VMEM((NZ, 8, H), f32),
-            pltpu.VMEM((2, MODES, W, W), f32),
             pltpu.SemaphoreType.DMA((7,)),
             pltpu.SemaphoreType.DMA((n_sems,)),
             pltpu.SemaphoreType.DMA((n_sems,)),
@@ -934,13 +925,10 @@
     return pl.pallas_call(
         write_out,
         out_shape=shapes,
-        in_specs=[any_spec] * 4,
+        in_specs=[pl.BlockSpec(memory_space=pl.ANY)] * 2,
         out_specs=(any_spec,) * 4,
-        scratch_shapes=[
-            pltpu.VMEM((2, H, H), f32),
-            pltpu.VMEM((2, MODES, W, W), f32),
-            pltpu.SemaphoreType.DMA((2, 2 + 2 * MODES)),
-        ],
+        scratch_shapes=[pltpu.SemaphoreType.DMA((4,))],
+        compiler_params=pltpu.CompilerParams(vmem_limit_bytes=1 << 20),
     )(*results)
 
 

time: 119 us -> 113 us (0.950)
  Pallas kernels: 118 us -> 112 us
    pallas_call x2, Pallas kernels: 118 us -> 112 us  [the longest x1 111 us: local(): pl.pallas_call(functools.partial(kernel, n_row, n_col), out_shape=(pltpu....]
where the time goes in v4:
time: 113 us
  Pallas kernels  112 us (99%)
    pallas_call x1, Pallas kernels, local(): pl.pallas_call(functools.partial(kernel, n_row, n_col), out_shape=(pltpu....  111 us

profile of v4, /device:TPU:1, one launch (start us, length us, event | category | flops | bytes accessed | tf_op | source)
XLA Modules:
  0.0 112.7 jit_solution(10384746221509479174)
XLA Ops:
  0.6 110.7 %shard_map.111 = (f32[2,128,128]{2,1,0:T(8,128)S(1)}, f32[2,4,256,256]{3,2,1,0:T(8,128)S(1)}) custom-call(s32[1,2]{1,0:T(1,128)} %bitcast.3, f32[128,128]{1,0:T(8,128)} %ore_ref.1, f32[128,128]{1,0:T(8,128)} %oim_ref.1, f32[4,256,256]{2,1,0:T(8,128)} %pre_ref.1, f32[4,256,256]{2,1,0:T(8,128)} %pim_ref.1, f32[256,256]{1,0:T(8,128)} %bitcast.2, ...), custom_call_target="tpu_custom_call" | custom-call | tf_op jit(solution)/shard_map/pallas_call | solution.py:866
  111.3 1.4 %shard_map.112 = (f32[128,128]{1,0:T(8,128)}, f32[128,128]{1,0:T(8,128)}, f32[4,256,256]{2,1,0:T(8,128)}, f32[4,256,256]{2,1,0:T(8,128)}) custom-call(f32[2,128,128]{2,1,0:T(8,128)S(1)} %get-tuple-element.6.tile, f32[2,4,256,256]{3,2,1,0:T(8,128)S(1)} %get-tuple-element.7.af), custom_call_target="tpu_custom_call" | custom-call | tf_op jit(solution)/shard_map/pallas_call | solution.py:925

commit v5 on v4

--- a/solution.py
+++ b/solution.py
@@ -33,7 +33,8 @@
     imag = -np.sin(angle) / math.sqrt(W)
     right = np.block([[real, imag], [-imag, real]])
     left = np.block([[real, -imag], [imag, real]])
-    return (right.astype(np.float32).astype(bf16), left.astype(np.float32).astype(bf16))
+    order = np.arange(2 * W).reshape(2, 2, H).transpose(1, 0, 2).reshape(-1)
+    return tuple(t.astype(np.float32).astype(bf16) for t in (right, left, right[order]))
 
 
 class Sems:
@@ -62,10 +63,10 @@
     at["mass"] = sems.take(small + 1)
     at["rs_core"] = sems.take(4)
     at["rs_f"] = sems.take(12)
-    at["rs_g"] = sems.take(12)
+    at["rs_g"] = sems.take(6)
     at["rs_z"] = sems.take(NZ)
     at["ag_z"] = sems.take(NZ)
-    at["ag_g"] = sems.take(12)
+    at["ag_g"] = sems.take(6)
     at["ag_f"] = sems.take(12)
     at["ag_core"] = sems.take(4)
     return small, at, sems.count
@@ -82,6 +83,7 @@
     amp_ref,
     m1_ref,
     m2_ref,
+    m3_ref,
     tile,
     af,
     probe,
@@ -89,6 +91,7 @@
     amps,
     m1,
     m2,
+    m3,
     win,
     grad,
     psi,
@@ -205,6 +208,7 @@
         pltpu.make_async_copy(m1_ref, m1, load_sem.at[4]),
         pltpu.make_async_copy(m2_ref, m2, load_sem.at[5]),
         pltpu.make_async_copy(amp_ref, amps, load_sem.at[6]),
+        pltpu.make_async_copy(m3_ref, m3, load_sem.at[7]),
     ]
     for load in loads:
         load.start()
@@ -304,6 +308,10 @@
 
     def small_next(which, g, op):
         small_start(which, g + 1, small_finish(which, g, op))
+
+    def fold_sent():
+        for pair in fold_a + [fold_b] + fold_r:
+            pair.sent()
 
     def halo_start():
         for pair in halo_r:
@@ -336,9 +344,6 @@
             for c in range(2):
                 win[c, rows, :H] = jnp.where(right_of[rows], hh[1, 0, c, rows], hh[0, 0, c, rows])
             half_block(n)
-        for pair in halo_r + [halo_o] + halo_s:
-            pair.sent()
-
     def half_block(b):
         for r in range(0, Q, step_rows):
             here = slice(b * Q + r, b * Q + r + step_rows)
@@ -368,6 +373,14 @@
             for m in range(MODES):
                 hs[m, part * W : (part + 1) * W] = out[m * W : (m + 1) * W]
 
+    def exits(part, modes=range(MODES)):
+        rows = slice(part * W, (part + 1) * W)
+        for m in modes:
+            spec[m, rows] = jnp.dot(m3[rows, :], hs[m], preferred_element_type=f32)
+
+    def re_at(r):
+        return r if r < H else r + H
+
     def product_left(table, modes=range(MODES)):
         for m in modes:
             spec[m] = jnp.dot(table[...], hs[m], preferred_element_type=f32)
@@ -393,25 +406,30 @@
     def make_grad(rows):
         for r in range(rows.start, rows.stop, step_rows):
             here = slice(r, r + step_rows)
-            here_im = slice(W + r, W + r + step_rows)
+            at_re = slice(re_at(r), re_at(r) + step_rows)
+            at_im = slice(re_at(r) + H, re_at(r) + H + step_rows)
             g_re = jnp.zeros((step_rows, W), f32)
             g_im = jnp.zeros((step_rows, W), f32)
             for m in range(MODES):
                 pr, pi = prot[m, here, :], prot[MODES + m, here, :]
-                er, ei = spec[m, here, :], spec[m, here_im, :]
+                er, ei = spec[m, at_re, :], spec[m, at_im, :]
                 g_re = g_re + (pr * er + pi * ei)
                 g_im = g_im + (pr * ei - pi * er)
             grad[0, here, :] = g_re
             grad[1, here, :] = g_im
 
-    def fold_start():
+    def fold_start(with_exits=True):
         zero = jnp.zeros((H, H), f32)
+        if with_exits:
+            exits(0)
         for n, rows in enumerate(rows_of):
             make_grad(rows)
             for c in range(2):
                 fs[0, 0, c, rows] = jnp.where(right_of[rows], zero[rows], grad[c, rows, :H])
                 fs[1, 0, c, rows] = jnp.where(right_of[rows], grad[c, rows, :H], zero[rows])
             fold_a[n].start()
+        if with_exits:
+            exits(1)
         make_grad(slice(H, W))
         for c in range(2):
             fs[0, 1, c] = jnp.where(right_of, zero, grad[c, H:, :H])
@@ -420,6 +438,8 @@
 
     def fold_middle(first=nothing):
         first()
+        for pair in halo_r + [halo_o] + halo_s:
+            pair.sent()
         for n, rows in enumerate(rows_of):
             fold_a[n].recv()
             here = rows_i[rows]
@@ -435,7 +455,7 @@
                 us[1, c, rows] = down
             fold_r[n].start()
 
-    def fold_finish(denom, again):
+    def fold_finish(inverse, again):
         fold_b.recv()
         for n, rows in enumerate(rows_of):
             own = slice(H + rows.start, H + rows.stop)
@@ -443,14 +463,11 @@
             fold_r[n].recv()
             for c in range(2):
                 total = sides[c] + ur[0, c, rows] + ur[1, c, rows]
-                tile[c, rows] = tile[c, rows] + total / denom[rows]
+                tile[c, rows] = tile[c, rows] + total * inverse[rows]
             if again:
                 halo_r[n].start()
         if again:
             halo_o.start()
-        for pair in fold_a + [fold_b] + fold_r:
-            pair.sent()
-
     pos_h.start()
     pos_r.start()
     loads[0].wait()
@@ -540,23 +557,22 @@
         make_change()
         product_right(m2)
         first()
-        product_left(m1)
 
     halo_to_half(settle_light, lambda: small_next(0, 0, jnp.maximum))
     transforms(lambda: small_next(0, 1, jnp.maximum))
     fold_start()
     fold_middle(lambda: small_next(0, 2, jnp.maximum))
     peak = small_finish(0, 3, jnp.maximum)
-    light[...] = light[...] + light_ratio * jnp.max(peak)
+    light[...] = 1.0 / (light[...] + light_ratio * jnp.max(peak))
     fold_finish(light[...], True)
 
-    halo_to_half()
+    halo_to_half(fold_sent)
     transforms()
     fold_start()
     fold_middle()
     fold_finish(light[...], True)
 
-    halo_to_half()
+    halo_to_half(fold_sent)
     spot = 4 * f + g
 
     def mass_copies(stage):
@@ -638,8 +654,9 @@
             for b in range(4):
                 here = block(b)
                 here_im = slice(W + b * Q, W + b * Q + Q)
+                at_re = re_at(b * Q)
                 wr, wi = win[0, here, :], win[1, here, :]
-                er, ei = spec[m, here, :], spec[m, here_im, :]
+                er, ei = spec[m, at_re : at_re + Q, :], spec[m, at_re + H : at_re + H + Q, :]
                 prod[m, here, :] = wr * er + wi * ei
                 prod[m, here_im, :] = wr * ei - wi * er
             return carry
@@ -668,12 +685,12 @@
         remote(w_sib.at[k], r_core.at[k], at["rs_core"] + k, at["rs_core"] + k, sibling)
         for k in range(4)
     ]
-    product_left(m1, [2 * sib, 2 * sib + 1])
+    product_left(m3, [2 * sib, 2 * sib + 1])
     mode_products(sib)
     for k in range(4):
         put_part(w_sib, k, sib)
         rs_core[k].start()
-    product_left(m1, [2 * core, 2 * core + 1])
+    product_left(m3, [2 * core, 2 * core + 1])
     mode_products(core)
 
     def rs_f(k):
@@ -685,10 +702,13 @@
             for q in range(1, 4)
         ]
 
-    def rs_g(k):
-        first = at["rs_g"] + 3 * k - 1
+    def rs_g(half):
+        first = at["rs_g"] + 3 * half - 1
+        parts = pl.ds(2 * half, 2)
         return [
-            remote(w_own.at[k, 4 * f + g_at[q]], r_g.at[k, q - 1], first + q, first + q, g_dev[q])
+            remote(
+                w_own.at[parts, 4 * f + g_at[q]], r_g.at[half, q - 1], first + q, first + q, g_dev[q]
+            )
             for q in range(1, 4)
         ]
 
@@ -716,7 +736,7 @@
         lax.fori_loop(0, 16, add_core, 0, unroll=4)
         for copy in rs_f(k):
             copy.start()
-    fold_start()
+    fold_start(False)
     mass_next(1)
     fold_middle()
     for k in range(4):
@@ -724,16 +744,27 @@
             copy.wait_recv()
         mine = pl.ds(4 * f, 4)
         w_own[k, mine] = w_own[k, mine] + (r_f[k, 0] + r_f[k, 1] + r_f[k, 2])
-        for copy in rs_g(k):
-            copy.start()
+        if k % 2:
+            for copy in rs_g(k // 2):
+                copy.start()
     mass_next(2)
     fold_finish(light[...], False)
+    for half in range(2):
+        for copy in rs_g(half):
+            copy.wait_recv()
+        for k in (2 * half, 2 * half + 1):
+            w_own[k, spot] = w_own[k, spot] + (
+                r_g[half, 0, k % 2] + r_g[half, 1, k % 2] + r_g[half, 2, k % 2]
+            )
+            for mode in range(2):
+                pl.when(z != 2 * k + mode)(rs_z(k, mode).start)
     for k in range(4):
-        for copy in rs_g(k):
-            copy.wait_recv()
-        w_own[k, spot] = w_own[k, spot] + (r_g[k, 0] + r_g[k, 1] + r_g[k, 2])
-        for mode in range(2):
-            pl.when(z != 2 * k + mode)(rs_z(k, mode).start)
+        rs_core[k].wait_send()
+        for copy in rs_f(k):
+            copy.wait_send()
+    for half in range(2):
+        for copy in rs_g(half):
+            copy.wait_send()
 
     part = z // 2
     mode = lax.rem(z, 2)
@@ -745,17 +776,19 @@
     mean_mass = jnp.sum(small_finish(1, 3, jnp.add)) / (W * W)
     scale = probe_step / (mass_here + mass_ratio * mean_mass)
 
-    def spot_rows(k, n):
-        start = k * Q
-        if n <= 32:
-            start = start + lax.rem(f, 2) * 32
-        if n <= 8:
-            start = start + g * 8
-        return pl.ds(pl.multiple_of(start, 8), n)
-
-    lanes = pl.ds(pl.multiple_of((f // 2) * H, H), H)
-    at_row = spot_rows(part, 8)
+    def rows_in_part(n, f_of, g_of):
+        start = lax.rem(f_of, 2) * 32
+        if n == 8:
+            start = start + g_of * 8
+        return pl.ds(pl.multiple_of(start, n), n)
+
+    def lanes_of(f_of):
+        return pl.ds(pl.multiple_of((f_of // 2) * H, H), H)
+
+    lanes = lanes_of(f)
+    mine_8 = rows_in_part(8, f, g)
     m = 2 * core + mode
+    at_row = pl.ds(pl.multiple_of(part * Q + lax.rem(f, 2) * 32 + g * 8, 8), 8)
     old_re = probe[m, at_row, lanes]
     old_im = probe[MODES + m, at_row, lanes]
     for k in range(nz):
@@ -765,83 +798,74 @@
     for k in range(1, nz):
         g_re = g_re + r_z[k, 0]
         g_im = g_im + r_z[k, 1]
-    af[0, m, at_row, lanes] = old_re + g_re * scale
-    af[1, m, at_row, lanes] = old_im + g_im * scale
+    af[0, m, part, mine_8, lanes] = old_re + g_re * scale
+    af[1, m, part, mine_8, lanes] = old_im + g_im * scale
 
     both = pl.ds(2 * core, 2)
 
     def ag_z(to):
-        where = af.at[:, m, at_row, lanes]
+        where = af.at[:, m, part, mine_8, lanes]
         return remote(where, where, at["ag_z"] + to, at["ag_z"] + z, dev_at(x, y, to, core))
 
     def ag_z_from(k):
-        where = af.at[:, 2 * core + k % 2, spot_rows(k // 2, 8), lanes]
+        where = af.at[:, 2 * core + k % 2, k // 2, mine_8, lanes]
         return remote(where, where, at["ag_z"] + k, at["ag_z"] + k, dev_at(x, y, k, core))
 
-    def ag_g(k):
-        where = af.at[:, both, spot_rows(k, 8), lanes]
-        first = at["ag_g"] + 3 * k - 1
-        return [remote(where, where, first + q, first + q, g_dev[q]) for q in range(1, 4)]
-
-    def ag_g_from(k):
-        first = at["ag_g"] + 3 * k - 1
+    def ag_g(half, arriving):
+        first = at["ag_g"] + 3 * half - 1
         copies = []
         for q in range(1, 4):
-            start = k * Q + lax.rem(f, 2) * 32 + g_at[q] * 8
-            where = af.at[:, both, pl.ds(pl.multiple_of(start, 8), 8), lanes]
+            rows = rows_in_part(8, f, g_at[q] if arriving else g)
+            where = af.at[:, both, pl.ds(2 * half, 2), rows, lanes]
             copies.append(remote(where, where, first + q, first + q, g_dev[q]))
         return copies
 
-    def ag_f(k):
-        where = af.at[:, both, spot_rows(k, 32), lanes]
-        first = at["ag_f"] + 3 * k - 1
-        return [remote(where, where, first + q, first + q, f_dev[q]) for q in range(1, 4)]
-
-    def ag_f_from(k):
+    def ag_f(k, arriving):
         first = at["ag_f"] + 3 * k - 1
         copies = []
         for q in range(1, 4):
-            start = k * Q + lax.rem(f_at[q], 2) * 32
-            where = af.at[
-                :,
-                both,
-                pl.ds(pl.multiple_of(start, 32), 32),
-                pl.ds(pl.multiple_of((f_at[q] // 2) * H, H), H),
-            ]
+            f_of = f_at[q] if arriving else f
+            where = af.at[:, both, k, rows_in_part(32, f_of, g), lanes_of(f_of)]
             copies.append(remote(where, where, first + q, first + q, f_dev[q]))
         return copies
 
     def ag_core(k, which):
-        where = af.at[:, pl.ds(2 * which, 2), k * Q : (k + 1) * Q]
+        where = af.at[:, pl.ds(2 * which, 2), k]
         index = at["ag_core"] + k
         return remote(where, where, index, index, sibling)
 
     for k in range(nz):
         pl.when(z != k)(ag_z(k).start)
+    for k in range(nz):
+        pl.when(z != k)(rs_z(k // 2, k % 2).wait_send)
+    for half in range(2):
+        for k in range(4 * half, 4 * half + 4):
+            pl.when(z != k)(ag_z_from(k).wait_recv)
+        for copy in ag_g(half, False):
+            copy.start()
+    for k in range(nz):
+        pl.when(z != k)(ag_z(k).wait_send)
+    for half in range(2):
+        for copy in ag_g(half, True):
+            copy.wait_recv()
+        for k in (2 * half, 2 * half + 1):
+            for copy in ag_f(k, False):
+                copy.start()
+    for half in range(2):
+        for copy in ag_g(half, False):
+            copy.wait_send()
     for k in range(4):
-        for mode_k in range(2):
-            pl.when(z != 2 * k + mode_k)(ag_z_from(2 * k + mode_k).wait_recv)
-        for copy in ag_g(k):
-            copy.start()
-    for k in range(4):
-        for copy in ag_g_from(k):
-            copy.wait_recv()
-        for copy in ag_f(k):
-            copy.start()
-    for k in range(4):
-        for copy in ag_f_from(k):
+        for copy in ag_f(k, True):
             copy.wait_recv()
         ag_core(k, core).start()
     for k in range(4):
+        for copy in ag_f(k, False):
+            copy.wait_send()
+    fold_sent()
+    for k in range(4):
         ag_core(k, sib).wait_recv()
     for k in range(4):
-        rs_core[k].wait_send()
         ag_core(k, core).wait_send()
-        for copy in rs_f(k) + rs_g(k) + ag_g(k) + ag_f(k):
-            copy.wait_send()
-    for k in range(nz):
-        pl.when(z != k)(rs_z(k // 2, k % 2).wait_send)
-        pl.when(z != k)(ag_z(k).wait_send)
 
 
 def write_out(tile, af, new_re, new_im, new_pre, new_pim, sem):
@@ -855,23 +879,24 @@
 
 def local(n_row, n_col, obj_re, obj_im, probe_re, probe_im, amps, positions):
     n_small, at, n_sems = layout()
-    right, left = make_pairs()
+    right, left, right_rows = make_pairs()
     any_spec = pl.BlockSpec(memory_space=pltpu.HBM)
     shapes = (
         jax.ShapeDtypeStruct((H, H), f32),
         jax.ShapeDtypeStruct((H, H), f32),
-        jax.ShapeDtypeStruct((MODES, W, W), f32),
-        jax.ShapeDtypeStruct((MODES, W, W), f32),
+        jax.ShapeDtypeStruct((MODES, 4, Q, W), f32),
+        jax.ShapeDtypeStruct((MODES, 4, Q, W), f32),
     )
     results = pl.pallas_call(
         functools.partial(kernel, n_row, n_col),
-        out_shape=(pltpu.VMEM((2, H, H), f32), pltpu.VMEM((2, MODES, W, W), f32)),
-        in_specs=[pl.BlockSpec(memory_space=pltpu.SMEM)] + [any_spec] * 7,
+        out_shape=(pltpu.VMEM((2, H, H), f32), pltpu.VMEM((2, MODES, 4, Q, W), f32)),
+        in_specs=[pl.BlockSpec(memory_space=pltpu.SMEM)] + [any_spec] * 8,
         out_specs=(pl.BlockSpec(memory_space=pltpu.VMEM),) * 2,
         scratch_shapes=[
             pltpu.VMEM((2 * MODES, W, W), f32),
             pltpu.VMEM((2 * MODES, W, W), f32),
             pltpu.VMEM((W, W), f32),
+            pltpu.VMEM((2 * W, 2 * W), bf16),
             pltpu.VMEM((2 * W, 2 * W), bf16),
             pltpu.VMEM((2 * W, 2 * W), bf16),
             pltpu.VMEM((2, W, W), f32),
@@ -898,14 +923,14 @@
             pltpu.VMEM((4, 16, 4, 8, H), f32),
             pltpu.VMEM((4, 16, 4, 8, H), f32),
             pltpu.VMEM((4, 3, 4, 4, 8, H), f32),
-            pltpu.VMEM((4, 3, 4, 8, H), f32),
+            pltpu.VMEM((2, 3, 2, 4, 8, H), f32),
             pltpu.VMEM((NZ, 2, 8, H), f32),
             pltpu.VMEM((2, 4, 16, 8, H), f32),
             pltpu.VMEM((4, 16, 8, H), f32),
             pltpu.VMEM((3, 4, 4, 8, H), f32),
             pltpu.VMEM((3, 4, 1, 8, H), f32),
             pltpu.VMEM((NZ, 8, H), f32),
-            pltpu.SemaphoreType.DMA((7,)),
+            pltpu.SemaphoreType.DMA((8,)),
             pltpu.SemaphoreType.DMA((n_sems,)),
             pltpu.SemaphoreType.DMA((n_sems,)),
         ],
@@ -921,8 +946,9 @@
         amps.reshape(W, W),
         jnp.asarray(right),
         jnp.asarray(left),
+        jnp.asarray(right_rows),
     )
-    return pl.pallas_call(
+    new_re, new_im, new_pre, new_pim = pl.pallas_call(
         write_out,
         out_shape=shapes,
         in_specs=[pl.BlockSpec(memory_space=pl.ANY)] * 2,
@@ -930,6 +956,7 @@
         scratch_shapes=[pltpu.SemaphoreType.DMA((4,))],
         compiler_params=pltpu.CompilerParams(vmem_limit_bytes=1 << 20),
     )(*results)
+    return (new_re, new_im, new_pre.reshape(MODES, W, W), new_pim.reshape(MODES, W, W))
 
 
 def solution(mesh):

time: 113 us -> 113 us (level)
  no operation moved by 1% of the time
where the time goes in v5:
time: 113 us
  Pallas kernels  112 us (99%)
    pallas_call x1, Pallas kernels, local(): pl.pallas_call(functools.partial(kernel, n_row, n_col), out_shape=(pltpu....  111 us

profile of v5, /device:TPU:1, one launch (start us, length us, event | category | flops | bytes accessed | tf_op | source)
XLA Modules:
  0.0 113.1 jit_solution(13309406935448851758)
XLA Ops:
  0.6 111.0 %shard_map.120 = (f32[2,128,128]{2,1,0:T(8,128)S(1)}, f32[2,4,4,64,256]{4,3,2,1,0:T(8,128)S(1)}) custom-call(s32[1,2]{1,0:T(1,128)} %bitcast.5, f32[128,128]{1,0:T(8,128)} %ore_ref.1, f32[128,128]{1,0:T(8,128)} %oim_ref.1, f32[4,256,256]{2,1,0:T(8,128)} %pre_ref.1, f32[4,256,256]{2,1,0:T(8,128)} %pim_ref.1, f32[256,256]{1,0:T(8,128)} %bitcast.4, ...), custom_call_target="tpu_custom_call" | custom-call | tf_op jit(solution)/shard_map/pallas_call | solution.py:890
  111.7 1.4 %shard_map.121 = (f32[128,128]{1,0:T(8,128)}, f32[128,128]{1,0:T(8,128)}, f32[4,4,64,256]{3,2,1,0:T(8,128)}, f32[4,4,64,256]{3,2,1,0:T(8,128)}) custom-call(f32[2,128,128]{2,1,0:T(8,128)S(1)} %get-tuple-element.10.tile, f32[2,4,4,64,256]{4,3,2,1,0:T(8,128)S(1)} %get-tuple-element.11.af), custom_call_target="tpu_custom_call" | custom-call | tf_op jit(solution)/shard_map/pallas_call | solution.py:951

commit v6 on v5

--- a/solution.py
+++ b/solution.py
@@ -54,6 +54,8 @@
 def layout():
     sems = Sems()
     at = {}
+    for name in ("move", "back"):
+        at[name] = sems.take(3)
     for name in ("pos_h", "pos_r", "pos_c", "halo_o", "fold_b"):
         at[name] = sems.take(2)
     for name in ("halo_r", "halo_s", "fold_a", "fold_r"):
@@ -84,8 +86,11 @@
     m1_ref,
     m2_ref,
     m3_ref,
+    new_tile,
+    af,
     tile,
-    af,
+    tile0,
+    pos0,
     probe,
     prot,
     amps,
@@ -161,14 +166,39 @@
     z_at = [lax.rem(z + k, nz) for k in range(nz)]
     z_dev = [dev_at(x, y, z_at[k], core) for k in range(nz)]
 
-    has = {
-        "v": [row > 0, row < n_row - 1],
-        "h": [col > 0, col < n_col - 1],
-    }
-    near = {
-        "v": [(jnp.maximum(row - 1, 0), col), (jnp.minimum(row + 1, n_row - 1), col)],
-        "h": [(row, jnp.maximum(col - 1, 0)), (row, jnp.minimum(col + 1, n_col - 1))],
-    }
+    def worker(tile_row, tile_col):
+        high = tile_row // nz
+        low = lax.rem(tile_col // 2, 2)
+        turn = lax.rem(tile_col // 4 + high, 2)
+        return (tile_row, tile_col + 2 * turn * (1 - 2 * low))
+
+    moved = lax.rem(y + row // nz, 2) == 1
+    mate = worker(row, col)
+    my_col = mate[1]
+
+    def sides(tile_row, tile_col, place):
+        has = {
+            "v": [tile_row > 0, tile_row < n_row - 1],
+            "h": [tile_col > 0, tile_col < n_col - 1],
+        }
+        near = {
+            "v": [
+                place(jnp.maximum(tile_row - 1, 0), tile_col),
+                place(jnp.minimum(tile_row + 1, n_row - 1), tile_col),
+            ],
+            "h": [
+                place(tile_row, jnp.maximum(tile_col - 1, 0)),
+                place(tile_row, jnp.minimum(tile_col + 1, n_col - 1)),
+            ],
+        }
+        return has, near
+
+    def itself(tile_row, tile_col):
+        return (tile_row, tile_col)
+
+    has, near = sides(row, my_col, worker)
+    has0, near0 = sides(row, col, worker)
+    _, from0 = sides(row, my_col, itself)
 
     def remote(src, dst, index_send, index_recv, dev):
         return pltpu.make_async_remote_copy(
@@ -181,16 +211,17 @@
         )
 
     class Pair:
-        def __init__(self, axis, srcs, dst_of, first):
+        def __init__(self, axis, srcs, dst_of, first, has_out=None, near_out=None):
             self.axis = axis
+            self.has_out = (has_out or has)[axis]
             self.copies = [
-                remote(srcs[d], dst_of(1 - d), first + d, first + 1 - d, near[axis][d])
+                remote(srcs[d], dst_of(1 - d), first + d, first + 1 - d, (near_out or near)[axis][d])
                 for d in range(2)
             ]
 
         def start(self, d=None):
             for side in (0, 1) if d is None else (d,):
-                pl.when(has[self.axis][side])(self.copies[side].start)
+                pl.when(self.has_out[side])(self.copies[side].start)
 
         def recv(self, d=None):
             for side in (0, 1) if d is None else (d,):
@@ -198,25 +229,24 @@
 
         def sent(self):
             for side in (0, 1):
-                pl.when(has[self.axis][side])(self.copies[side].wait_send)
+                pl.when(self.has_out[side])(self.copies[side].wait_send)
 
     loads = [
-        pltpu.make_async_copy(ore_ref, tile.at[0], load_sem.at[0]),
-        pltpu.make_async_copy(oim_ref, tile.at[1], load_sem.at[1]),
+        pltpu.make_async_copy(ore_ref, tile0.at[0], load_sem.at[0]),
+        pltpu.make_async_copy(oim_ref, tile0.at[1], load_sem.at[1]),
         pltpu.make_async_copy(pre_ref, probe.at[pl.ds(0, MODES)], load_sem.at[2]),
         pltpu.make_async_copy(pim_ref, probe.at[pl.ds(MODES, MODES)], load_sem.at[3]),
         pltpu.make_async_copy(m1_ref, m1, load_sem.at[4]),
         pltpu.make_async_copy(m2_ref, m2, load_sem.at[5]),
-        pltpu.make_async_copy(amp_ref, amps, load_sem.at[6]),
-        pltpu.make_async_copy(m3_ref, m3, load_sem.at[7]),
+        pltpu.make_async_copy(m3_ref, m3, load_sem.at[6]),
     ]
     for load in loads:
         load.start()
+    amps_here = pltpu.make_async_copy(amp_ref, amps, load_sem.at[7])
+    pl.when(jnp.logical_not(moved))(amps_here.start)
 
     a_r = (pos_ref[0, 0] - (row * H - H)) // Q
     a_c = (pos_ref[0, 1] - (col * H - H)) // Q
-    lr = a_r * Q
-    lc = a_c * Q
 
     hv[...] = jnp.zeros_like(hv)
     hh[...] = jnp.zeros_like(hh)
@@ -226,34 +256,35 @@
         for di in range(3):
             posb[dj, di] = jnp.full((8, 128), 4 * di + dj, jnp.int32)
     posh[...] = jnp.zeros_like(posh)
-    posb[1, 1] = jnp.broadcast_to(4 * a_r + a_c, (8, 128)).astype(jnp.int32)
+    code0 = jnp.broadcast_to(4 * a_r + a_c, (8, 128)).astype(jnp.int32)
+    pos0[...] = code0
+    posb[1, 1] = code0
 
     barrier = pltpu.get_barrier_semaphore()
     always = [sibling] + f_dev[1:] + g_dev[1:] + z_dev[1:]
     for dev in always:
         pl.semaphore_signal(barrier, inc=1, device_id=dev, device_id_type=MESH)
-    expected = len(always)
+    expected = len(always) + moved.astype(jnp.int32)
+
+    def greet(dev):
+        pl.semaphore_signal(barrier, inc=1, device_id=dev, device_id_type=MESH)
+
+    pl.when(moved)(lambda: greet(mate))
     for axis in ("v", "h"):
         for d in range(2):
-
-            def greet(axis=axis, d=d):
-                pl.semaphore_signal(barrier, inc=1, device_id=near[axis][d], device_id_type=MESH)
-
-            pl.when(has[axis][d])(greet)
-            expected = expected + has[axis][d].astype(jnp.int32)
+            pl.when(has[axis][d])(lambda axis=axis, d=d: greet(near[axis][d]))
+            pl.when(has[axis][d])(lambda axis=axis, d=d: greet(from0[axis][d]))
+            expected = expected + has[axis][d].astype(jnp.int32) + has0[axis][d].astype(jnp.int32)
     pl.semaphore_wait(barrier, expected)
 
     rows_i = lax.broadcasted_iota(jnp.int32, (H, H), 0)
     cols_i = lax.broadcasted_iota(jnp.int32, (H, H), 1)
-    below = rows_i < lr
-    right_of = cols_i < lc
-
-    pos_h = Pair("h", [posb.at[1, 1]] * 2, lambda d: posh.at[d], at["pos_h"])
-    pos_r = Pair("v", [posb.at[1, 1]] * 2, lambda d: posb.at[1, 2 * d], at["pos_r"])
+    pos_h = Pair("h", [pos0] * 2, lambda d: posh.at[d], at["pos_h"], has0, near0)
+    pos_r = Pair("v", [pos0] * 2, lambda d: posb.at[1, 2 * d], at["pos_r"], has0, near0)
     pos_c = Pair("h", [posb.at[1]] * 2, lambda d: posb.at[2 * d], at["pos_c"])
     rows_of = [slice(n * (H // CHUNKS), (n + 1) * (H // CHUNKS)) for n in range(CHUNKS)]
 
-    def chunked(axis, src_of, dst_of, first):
+    def chunked(axis, src_of, dst_of, first, has_out=None, near_out=None):
         pairs = []
         for n in range(CHUNKS):
             rows = pl.ds(n * (H // CHUNKS), H // CHUNKS)
@@ -263,10 +294,19 @@
                     [src_of(d).at[:, rows] for d in range(2)],
                     lambda d, rows=rows: dst_of(d).at[:, rows],
                     first + 2 * n,
+                    has_out,
+                    near_out,
                 )
             )
         return pairs
 
+    first_o = Pair("h", [tile0] * 2, lambda d: hh.at[d, 1], at["halo_o"], has0, near0)
+    first_r = chunked("v", lambda d: tile0, lambda d: hv.at[d], at["halo_r"], has0, near0)
+    move = at["move"]
+    move_pos = remote(pos0, posb.at[1, 1], move, move, mate)
+    move_tile = remote(tile0, tile, move + 1, move + 1, mate)
+    move_amps = remote(amp_ref, amps, move + 2, move + 2, mate)
+    move_back = remote(tile, new_tile, at["back"], at["back"], mate)
     halo_o = Pair("h", [tile] * 2, lambda d: hh.at[d, 1], at["halo_o"])
     halo_r = chunked("v", lambda d: tile, lambda d: hv.at[d], at["halo_r"])
     halo_s = chunked("h", lambda d: sh.at[d], lambda d: hh.at[d, 0], at["halo_s"])
@@ -276,6 +316,12 @@
 
     def near_lr(d):
         return (posh[d][0:1, :] // 4) * Q
+
+    def my_lr():
+        return (posb[1, 1][0:1, :] // 4) * Q
+
+    def my_lc():
+        return lax.rem(posb[1, 1][0:1, :], 4) * Q
 
     groups = [[sibling], f_dev[1:], g_dev[1:], z_dev[1:]]
     small_first = [0]
@@ -312,11 +358,6 @@
     def fold_sent():
         for pair in fold_a + [fold_b] + fold_r:
             pair.sent()
-
-    def halo_start():
-        for pair in halo_r:
-            pair.start()
-        halo_o.start()
 
     def nothing():
         pass
@@ -436,14 +477,14 @@
             fs[1, 1, c] = jnp.where(right_of, grad[c, H:, :H], zero)
         fold_b.start()
 
-    def fold_middle(first=nothing):
+    def fold_middle(first=nothing, opening=False):
         first()
-        for pair in halo_r + [halo_o] + halo_s:
+        for pair in (first_r + [first_o] if opening else halo_r + [halo_o]) + halo_s:
             pair.sent()
         for n, rows in enumerate(rows_of):
             fold_a[n].recv()
             here = rows_i[rows]
-            picks = [here < lr, here < near_lr(0), here < near_lr(1)]
+            picks = [here < my_lr(), here < near_lr(0), here < near_lr(1)]
             for c in range(2):
                 parts = [grad[c, rows, H:], fr[0, 0, c, rows], fr[1, 0, c, rows]]
                 up = jnp.zeros((H // CHUNKS, H), f32)
@@ -470,30 +511,15 @@
             halo_o.start()
     pos_h.start()
     pos_r.start()
+    pl.when(moved)(move_pos.start)
     loads[0].wait()
     loads[1].wait()
-    halo_start()
+    for pair in first_r:
+        pair.start()
+    first_o.start()
+    pl.when(moved)(move_tile.start)
     loads[2].wait()
     loads[3].wait()
-
-    def turned(three, back):
-        rows_by = jnp.broadcast_to(a_r, three[0].shape)
-        x = jnp.where(rows_by == 0, three[0], jnp.where(rows_by == 1, three[1], three[2]))
-        one = pltpu.roll(x, W - Q if back else Q, 1)
-        two = pltpu.roll(x, H, 1)
-        cols_by = jnp.broadcast_to(a_c, x.shape)
-        return jnp.where(cols_by == 0, x, jnp.where(cols_by == 1, one, two))
-
-    def block(b):
-        return slice((b % 4) * Q, (b % 4) * Q + Q)
-
-    for b in range(4):
-
-        def rotate(m, carry, b=b):
-            prot[m, block(b), :] = turned([probe[m, block(b - t), :] for t in range(3)], False)
-            return carry
-
-        lax.fori_loop(0, 2 * MODES, rotate, 0)
 
     padded[...] = jnp.zeros_like(padded)
     for b in range(4):
@@ -509,18 +535,56 @@
         rows = slice(b * Q, (b + 1) * Q)
         padded64[rows, :] = pltpu.roll(padded[rows, :], Q, 1)
 
+    pl.when(moved)(move_pos.wait_recv)
+    pos_r.recv()
+    pos_c.start()
+    pos_h.recv()
+    below = rows_i < my_lr()
+    right_of = cols_i < my_lc()
+    turns = jnp.concatenate([posb[1, 1][0:1, :]] * 2, axis=1)
+    a_r_row = turns // 4
+    a_c_row = lax.rem(turns, 4)
+
+    def turned(three, back):
+        rows_by = jnp.broadcast_to(a_r_row, three[0].shape)
+        x = jnp.where(rows_by == 0, three[0], jnp.where(rows_by == 1, three[1], three[2]))
+        one = pltpu.roll(x, W - Q if back else Q, 1)
+        two = pltpu.roll(x, H, 1)
+        cols_by = jnp.broadcast_to(a_c_row, x.shape)
+        return jnp.where(cols_by == 0, x, jnp.where(cols_by == 1, one, two))
+
+    def block(b):
+        return slice((b % 4) * Q, (b % 4) * Q + Q)
+
+    for b in range(4):
+
+        def rotate(m, carry, b=b):
+            prot[m, block(b), :] = turned([probe[m, block(b - t), :] for t in range(3)], False)
+            return carry
+
+        lax.fori_loop(0, 2 * MODES, rotate, 0)
+
     for load in loads[4:]:
         load.wait()
-    pos_h.recv()
-    pos_r.recv()
-    pos_c.start()
 
     def settle_light():
+        pl.when(moved)(move_amps.start)
         pos_c.recv()
         pos_h.sent()
         pos_r.sent()
         pos_c.sent()
+        pl.when(moved)(move_pos.wait_send)
         make_light()
+
+        def take_tile():
+            move_tile.wait_recv()
+            move_tile.wait_send()
+
+        def keep_tile():
+            tile[...] = tile0[...]
+
+        pl.when(moved)(take_tile)
+        pl.when(jnp.logical_not(moved))(keep_tile)
 
     def make_light():
         peak = jnp.full((8, H), 0.0, f32)
@@ -552,16 +616,25 @@
                 peak = jnp.maximum(peak, total[k * 8 : (k + 1) * 8, :])
         small_start(0, 0, peak)
 
-    def transforms(first=nothing):
+    def transforms(first=nothing, before=nothing):
         product_left(m2)
+        before()
         make_change()
         product_right(m2)
         first()
 
     halo_to_half(settle_light, lambda: small_next(0, 0, jnp.maximum))
-    transforms(lambda: small_next(0, 1, jnp.maximum))
+    def first_change():
+        def take_amps():
+            move_amps.wait_recv()
+            move_amps.wait_send()
+
+        pl.when(moved)(take_amps)
+        pl.when(jnp.logical_not(moved))(amps_here.wait)
+
+    transforms(lambda: small_next(0, 1, jnp.maximum), first_change)
     fold_start()
-    fold_middle(lambda: small_next(0, 2, jnp.maximum))
+    fold_middle(lambda: small_next(0, 2, jnp.maximum), True)
     peak = small_finish(0, 3, jnp.maximum)
     light[...] = 1.0 / (light[...] + light_ratio * jnp.max(peak))
     fold_finish(light[...], True)
@@ -749,6 +822,12 @@
                 copy.start()
     mass_next(2)
     fold_finish(light[...], False)
+
+    def keep_new():
+        new_tile[...] = tile[...]
+
+    pl.when(moved)(move_back.start)
+    pl.when(jnp.logical_not(moved))(keep_new)
     for half in range(2):
         for copy in rs_g(half):
             copy.wait_recv()
@@ -867,6 +946,12 @@
     for k in range(4):
         ag_core(k, core).wait_send()
 
+    def end_back():
+        move_back.wait_recv()
+        move_back.wait_send()
+
+    pl.when(moved)(end_back)
+
 
 def write_out(tile, af, new_re, new_im, new_pre, new_pim, sem):
     pairs = [(af.at[0], new_pre), (af.at[1], new_pim), (tile.at[0], new_re), (tile.at[1], new_im)]
@@ -893,6 +978,9 @@
         in_specs=[pl.BlockSpec(memory_space=pltpu.SMEM)] + [any_spec] * 8,
         out_specs=(pl.BlockSpec(memory_space=pltpu.VMEM),) * 2,
         scratch_shapes=[
+            pltpu.VMEM((2, H, H), f32),
+            pltpu.VMEM((2, H, H), f32),
+            pltpu.VMEM((8, H), jnp.int32),
             pltpu.VMEM((2 * MODES, W, W), f32),
             pltpu.VMEM((2 * MODES, W, W), f32),
             pltpu.VMEM((W, W), f32),

time: 113 us -> 118 us (1.044)
  Pallas kernels: 112 us -> 117 us
    pallas_call x1, Pallas kernels: 111 us -> 115 us  [local(): pl.pallas_call(functools.partial(kernel, n_row, n_col), out_shape=(pltpu....]
where the time goes in v6:
time: 118 us; the launch traced here: 117 us
  Pallas kernels  117 us (99%)
    pallas_call x1, Pallas kernels, local(): pl.pallas_call(functools.partial(kernel, n_row, n_col), out_shape=(pltpu....  115 us

profile of v6, /device:TPU:1, one launch (start us, length us, event | category | flops | bytes accessed | tf_op | source)
XLA Modules:
  0.0 117.5 jit_solution(6605479151728352838)
XLA Ops:
  0.6 115.5 %shard_map.120 = (f32[2,128,128]{2,1,0:T(8,128)S(1)}, f32[2,4,4,64,256]{4,3,2,1,0:T(8,128)S(1)}) custom-call(s32[1,2]{1,0:T(1,128)} %bitcast.5, f32[128,128]{1,0:T(8,128)} %ore_ref.1, f32[128,128]{1,0:T(8,128)} %oim_ref.1, f32[4,256,256]{2,1,0:T(8,128)} %pre_ref.1, f32[4,256,256]{2,1,0:T(8,128)} %pim_ref.1, f32[256,256]{1,0:T(8,128)} %bitcast.4, ...), custom_call_target="tpu_custom_call" | custom-call | tf_op jit(solution)/shard_map/pallas_call | solution.py:975
  116.1 1.4 %shard_map.121 = (f32[128,128]{1,0:T(8,128)}, f32[128,128]{1,0:T(8,128)}, f32[4,4,64,256]{3,2,1,0:T(8,128)}, f32[4,4,64,256]{3,2,1,0:T(8,128)}) custom-call(f32[2,128,128]{2,1,0:T(8,128)S(1)} %get-tuple-element.10.tile, f32[2,4,4,64,256]{4,3,2,1,0:T(8,128)S(1)} %get-tuple-element.11.af), custom_call_target="tpu_custom_call" | custom-call | tf_op jit(solution)/shard_map/pallas_call | solution.py:1039

commit v7 on v4

--- a/solution.py
+++ b/solution.py
@@ -463,7 +463,7 @@
         rows_by = jnp.broadcast_to(a_r, three[0].shape)
         x = jnp.where(rows_by == 0, three[0], jnp.where(rows_by == 1, three[1], three[2]))
         one = pltpu.roll(x, W - Q if back else Q, 1)
-        two = pltpu.roll(x, H, 1)
+        two = jnp.concatenate([x[:, H:], x[:, :H]], axis=1)
         cols_by = jnp.broadcast_to(a_c, x.shape)
         return jnp.where(cols_by == 0, x, jnp.where(cols_by == 1, one, two))
 
@@ -476,7 +476,7 @@
             prot[m, block(b), :] = turned([probe[m, block(b - t), :] for t in range(3)], False)
             return carry
 
-        lax.fori_loop(0, 2 * MODES, rotate, 0)
+        lax.fori_loop(0, 2 * MODES, rotate, 0, unroll=4)
 
     padded[...] = jnp.zeros_like(padded)
     for b in range(4):
@@ -718,7 +718,6 @@
             copy.start()
     fold_start()
     mass_next(1)
-    fold_middle()
     for k in range(4):
         for copy in rs_f(k):
             copy.wait_recv()
@@ -727,7 +726,7 @@
         for copy in rs_g(k):
             copy.start()
     mass_next(2)
-    fold_finish(light[...], False)
+    fold_middle()
     for k in range(4):
         for copy in rs_g(k):
             copy.wait_recv()
@@ -735,6 +734,7 @@
         for mode in range(2):
             pl.when(z != 2 * k + mode)(rs_z(k, mode).start)
 
+    fold_finish(light[...], False)
     part = z // 2
     mode = lax.rem(z, 2)
     r_z[z] = w_own[part, spot, pl.ds(2 * mode, 2)]

time: 113 us -> 113 us (level)
  no operation moved by 1% of the time
where the time goes in v7:
time: 113 us
  Pallas kernels  112 us (99%)
    pallas_call x1, Pallas kernels, local(): pl.pallas_call(functools.partial(kernel, n_row, n_col), out_shape=(pltpu....  111 us

profile of v7, /device:TPU:1, one launch (start us, length us, event | category | flops | bytes accessed | tf_op | source)
XLA Modules:
  0.0 113.0 jit_solution(275824573394781944)
XLA Ops:
  0.6 111.0 %shard_map.111 = (f32[2,128,128]{2,1,0:T(8,128)S(1)}, f32[2,4,256,256]{3,2,1,0:T(8,128)S(1)}) custom-call(s32[1,2]{1,0:T(1,128)} %bitcast.3, f32[128,128]{1,0:T(8,128)} %ore_ref.1, f32[128,128]{1,0:T(8,128)} %oim_ref.1, f32[4,256,256]{2,1,0:T(8,128)} %pre_ref.1, f32[4,256,256]{2,1,0:T(8,128)} %pim_ref.1, f32[256,256]{1,0:T(8,128)} %bitcast.2, ...), custom_call_target="tpu_custom_call" | custom-call | tf_op jit(solution)/shard_map/pallas_call | solution.py:866
  111.7 1.4 %shard_map.112 = (f32[128,128]{1,0:T(8,128)}, f32[128,128]{1,0:T(8,128)}, f32[4,256,256]{2,1,0:T(8,128)}, f32[4,256,256]{2,1,0:T(8,128)}) custom-call(f32[2,128,128]{2,1,0:T(8,128)S(1)} %get-tuple-element.6.tile, f32[2,4,256,256]{3,2,1,0:T(8,128)S(1)} %get-tuple-element.7.af), custom_call_target="tpu_custom_call" | custom-call | tf_op jit(solution)/shard_map/pallas_call | solution.py:925
